TPU v7x, 256 devices: a whole 4x4x8 slice. The times are simulated.
256 devices in a mesh: comp: 2 (over x_hi), gx: 64 (over z, y, core), gy: 2 (over x_lo).
Axes of the slice: x: 4 (x_hi: 2, x_lo: 2; x = x_hi * 2 + x_lo), y: 4, z: 8, core: 2. Of those that a mesh axis runs over, the one named last changes fastest.
Arguments:
- state: float32 [2, 2, 64, 1024, 256], P('comp', None, None, 'gx', 'gy'), may hold values from -6 to 6
- diffusion: float32 [2, 1024, 256], P('comp', 'gx', 'gy'), may hold values from 0.03 to 0.15
- vertical: float32 [2, 64], P('comp'), may hold values from 0.01 to 0.1
- coupling: float32 [2, 1024, 256], P('comp', 'gx', 'gy'), may hold values from 0.02 to 0.2
- land_sea: int32 [2, 1024, 256], P('comp', 'gx', 'gy'), may hold values 0 or 1
- route_tile: int32 [2, 128, 64, 1], P('comp', ('gx', 'gy')), may hold values from 0 to 127; in each aligned block of 64 rows (0 to 63, 64 to 127, ..., all dimensions but the last counted through in order) at most 2 rows name the same one
- route_src: int32 [2, 128, 64], P('comp', ('gx', 'gy')), may hold values from 0 to 15
- route_dst: int32 [2, 128, 64], P('comp', ('gx', 'gy')), may hold values from 0 to 15
- pair_cols: int32 [2, 128, 64], P('comp', ('gx', 'gy')), may hold values from 64 to 128
- intersection: bfloat16 [2, 128, 64, 128, 128], P('comp', ('gx', 'gy')), may hold values from 0 to 0.03125
Outputs:
- final_state: float32 [2, 2, 64, 1024, 256], P('comp', None, None, 'gx', 'gy')
Inputs may be any that keep to these rules, and one draw needn't show every extreme that they name: `route_tile`: within the 64 pairs of one component's tile no destination tile is named more than 2 times.
All inputs are finite; a program needn't handle non-finite values. No bound on the sum of `land_sea` on one device may be relied on, other than what follows from the above.
Results may differ from a plain program's by a relative error of at most 0.0003.
Values sent between devices are 32-bit elements; how exact they have to be, the bound alone decides.
No kernel may reach another device: no remote copies, remote signals or barrier semaphores. Data moves between devices by JAX's collectives and lax.ppermute only.
A program may use at most 128 MiB of HBM per device.

v0:
```python
import jax
import jax.numpy as jnp
from jax import lax
from jax.experimental import pallas as pl
from jax.experimental.pallas import tpu as pltpu
from jax.sharding import PartitionSpec as P

LANES = 128
LEV = 64
CX = 16
WIDE = 144
HALO = 6
CHUNK = 48
NEAR = 8
TALL = CX + 2 * NEAR
RING = 2 * LANES
NAT = 12
AXES = ("comp", "gx", "gy")
VMEM_LIMIT = 48 * 2**20

f32 = jnp.float32
VM = pl.BlockSpec(memory_space=pltpu.VMEM)
SM = pl.BlockSpec(memory_space=pltpu.SMEM)
HB = pl.BlockSpec(memory_space=pltpu.HBM)


def params():
    return pltpu.CompilerParams(vmem_limit_bytes=VMEM_LIMIT)


def struct(*shape):
    return jax.ShapeDtypeStruct(shape, f32)


def in_hbm(*arrays):
    return [pltpu.with_memory_space_constraint(a, pltpu.HBM) for a in arrays]


def exact_dot(a, b):
    return lax.dot_general(
        a, b, (((1,), (0,)), ((), ())), precision=lax.Precision.HIGHEST, preferred_element_type=f32
    )


PARTS = 4


def fetch_start(routes_hbm, routes, w_hbm, w, sems):
    for i in range(4):
        pltpu.make_async_copy(routes_hbm[i], routes[i], sems.at[i]).start()
    per = w.shape[0] // PARTS
    for i in range(PARTS):
        at = pl.ds(i * per, per)
        pltpu.make_async_copy(w_hbm.at[at], w.at[at], sems.at[4 + i]).start()


def write_contributions(routes_hbm, routes, w_hbm, w, sems, surf, count, put, mark):
    tile_ref, src_ref, dst_ref, cols_ref = routes
    for i in range(4):
        pltpu.make_async_copy(routes_hbm[i], routes[i], sems.at[i]).wait()

    def clear(i, c):
        count[i] = 0
        return c

    lax.fori_loop(0, count.shape[0], clear, 0)
    lanes = lax.broadcasted_iota(jnp.int32, (1, LANES), 1)
    per = w.shape[0] // PARTS
    for p in range(w.shape[0]):
        if p % per == 0:
            at = pl.ds(p, per)
            pltpu.make_async_copy(w_hbm.at[at], w.at[at], sems.at[4 + p // per]).wait()
        dest = tile_ref[p]
        slot = count[dest]
        count[dest] = slot + 1
        group = dest // 2
        part = dest - 2 * group
        picked = surf[pl.ds(pl.multiple_of(src_ref[p] * 8, 8), 8), :].astype(jnp.bfloat16)
        out = lax.dot_general(
            picked, w[p], (((1,), (1,)), ((), ())), preferred_element_type=f32
        )
        out = jnp.where(lanes < cols_ref[p], out, 0.0)
        put(group, part * 4 + slot * 2, out)
        if mark is not None:
            hot = (part * 2 + slot) * CX + dst_ref[p]
            mark(group, jnp.where(lanes == hot, 1.0, 0.0))


def pair_scratch(pairs, columns):
    return [pltpu.SMEM((pairs,), jnp.int32)] * 4 + [
        pltpu.VMEM((pairs, LANES, LANES), jnp.bfloat16),
        pltpu.VMEM((LANES, LANES), f32),
        pltpu.SMEM((2 * columns,), jnp.int32),
        pltpu.SemaphoreType.DMA((4 + PARTS,)),
    ]


def rounded(x):
    return x.astype(jnp.bfloat16).astype(f32)


def first_kernel(*refs):
    routes_hbm, w_hbm, state_hbm, send_ref = refs[:4], refs[4], refs[5], refs[6]
    routes, (w, surf, count, sems, top, top_sems) = refs[7:11], refs[11:]
    tops = [
        pltpu.make_async_copy(state_hbm.at[f, 0], top.at[f], top_sems.at[f]) for f in range(2)
    ]
    for copy in tops:
        copy.start()
    fetch_start(routes_hbm, routes, w_hbm, w, sems)
    send_ref[...] = jnp.zeros_like(send_ref)
    for f in range(2):
        tops[f].wait()
        surf[pl.ds(f, CX, stride=8), :] = rounded(top[f])

    def put(group, row, out):
        send_ref[group * 9 + row] = out[0:1]
        send_ref[group * 9 + row + 1] = out[1:2]

    def mark(group, value):
        send_ref[group * 9 + 8] += value

    write_contributions(routes_hbm, routes, w_hbm, w, sems, surf, count, put, mark)


def first_contributions(routes, weights, state, columns):
    pairs = weights.shape[0]
    return pl.pallas_call(
        first_kernel,
        in_specs=[HB] * 6,
        out_specs=VM,
        out_shape=struct(columns * 9, 1, LANES),
        scratch_shapes=pair_scratch(pairs, columns)
        + [pltpu.VMEM((2, CX, LANES), f32), pltpu.SemaphoreType.DMA((2,))],
        compiler_params=params(),
        name="contrib",
    )(*in_hbm(*routes, weights, state))


def prepare_kernel(
    info_ref, state_ref, diff_ref, coup_ref, sea_ref,
    cells_ref, nat_ref, low_ref, high_ref, side_ref, clow_ref, chigh_ref,
):
    sea = sea_ref[...].astype(f32)
    gate = jnp.where(info_ref[0] == 1, sea, jnp.ones_like(sea))
    coup = gate * coup_ref[...]
    nat_ref[0:16] = gate * diff_ref[...]
    nat_ref[16:32] = gate
    nat_ref[32:48] = coup
    nat_ref[48:64] = coup * sea
    for f in range(2):
        nat_ref[64 * (f + 1) : 64 * (f + 2)] = state_ref[f * LEV * CX : f * LEV * CX + 64]
    for x in range(CX):
        row = state_ref[pl.ds(x, LANES, stride=CX), :].T
        cells_ref[x] = row
        for j, piece in enumerate((row[0:8], row[120:128])):
            at = 16 * x + 8 * j
            side_ref[at : at + 8] = piece
            if x < HALO:
                clow_ref[at : at + 8] = piece
            if x >= CX - HALO:
                at -= 16 * (CX - HALO)
                chigh_ref[at : at + 8] = piece
        if x < HALO:
            low_ref[x * LANES : (x + 1) * LANES] = row
        if x >= CX - HALO:
            at = x - (CX - HALO)
            high_ref[at * LANES : (at + 1) * LANES] = row
    side_ref[16 * CX :] = nat_ref[...]
    for k in range(NAT):
        first = nat_ref[k * CX : k * CX + NEAR]
        final = nat_ref[(k + 1) * CX - NEAR : (k + 1) * CX]
        for ref, value, base in (
            (low_ref, first, HALO * LANES),
            (clow_ref, first, HALO * 16),
            (high_ref, final, HALO * LANES),
            (chigh_ref, final, HALO * 16),
        ):
            ref[base + k * NEAR : base + (k + 1) * NEAR] = value


def prepare(info, state, diffusion, coupling, land_sea):
    along = struct(HALO * LANES + NAT * NEAR, LANES)
    corner = struct(HALO * 16 + NAT * NEAR, LANES)
    return pl.pallas_call(
        prepare_kernel,
        in_specs=[SM] + [VM] * 4,
        out_specs=[VM] * 7,
        out_shape=[
            struct(CX, LANES, LANES), struct(NAT * CX, LANES),
            along, along, struct(16 * CX + NAT * CX, LANES), corner, corner,
        ],
        compiler_params=params(),
        name="prepare",
    )(info, state, diffusion, coupling, land_sea)


def linear_step(planes, made, mixing, diff, gate, damp):
    out = []
    for k in range(made):
        c = planes[k] if k < len(planes) else None
        vert = None

        def add(total, term):
            return term if total is None else total + term

        m = mixing[k]
        if k + 1 < len(planes):
            vert = add(vert, m * planes[k + 1])
        if k > 0:
            vert = add(vert, m * planes[k - 1])
        if c is None:
            out.append(gate * vert)
            continue
        vert = add(vert, -(m if k == 0 else 2.0 * m) * c)
        lap = (
            pltpu.roll(c, 1, 0) + pltpu.roll(c, TALL - 1, 0)
            + pltpu.roll(c, 1, 1) + pltpu.roll(c, RING - 1, 1) - 4.0 * c
        )
        new = c + (diff * lap + gate * vert)
        out.append(new - damp * c if k == 0 else new)
    return out


def coefs(coef_ref):
    return [coef_ref[k * TALL : (k + 1) * TALL] for k in range(4)]


def gather_kernel(mix_ref, nat_ref, low_ref, high_ref, side_ref, clow_ref, chigh_ref, coef_ref, top_ref):
    def plane(k):
        own = [high_ref[HALO * LANES + k * NEAR : HALO * LANES + (k + 1) * NEAR],
               nat_ref[k * CX : (k + 1) * CX],
               low_ref[HALO * LANES + k * NEAR : HALO * LANES + (k + 1) * NEAR]]
        other = [chigh_ref[HALO * 16 + k * NEAR : HALO * 16 + (k + 1) * NEAR],
                 side_ref[16 * CX + k * CX : 16 * CX + (k + 1) * CX],
                 clow_ref[HALO * 16 + k * NEAR : HALO * 16 + (k + 1) * NEAR]]
        return jnp.concatenate(
            [jnp.concatenate(own, axis=0), jnp.concatenate(other, axis=0)], axis=1
        )

    for k in range(4):
        coef_ref[k * TALL : (k + 1) * TALL] = plane(k)
    diff, gate, damp, _ = coefs(coef_ref)
    mixing = [mix_ref[k] for k in range(4)]
    for f in range(2):
        planes = [plane(4 + 4 * f + k) for k in range(4)]
        for made in (3, 2, 1):
            planes = linear_step(planes, made, mixing, diff, gate, damp)
        top_ref[f] = planes[0][NEAR : NEAR + CX, 0:LANES]


def gather(mixing, nat, halo):
    return pl.pallas_call(
        gather_kernel,
        in_specs=[SM] + [VM] * 6,
        out_specs=[VM] * 2,
        out_shape=[struct(4 * TALL, RING), struct(2, CX, LANES)],
        compiler_params=params(),
        name="gather",
    )(mixing, nat, *halo)


def forcing(info_ref, hops, coef_ref, work):
    a, b, l1, l2, h1, h2 = hops
    work[0 : 4 * NEAR] = l1[...] + l2[...]
    work[4 * NEAR : 4 * (NEAR + CX)] = a[...] + b[...]
    work[4 * (NEAR + CX) : 4 * TALL] = h1[...] + h2[...]
    north = info_ref[1] == 1
    scale = coef_ref[3 * TALL : 4 * TALL]
    out = []
    for f in range(2):
        one = work[pl.ds(f, TALL, stride=4), :]
        two = work[pl.ds(2 + f, TALL, stride=4), :]
        own = jnp.where(north, two, one)
        other = jnp.where(north, one, two)
        out.append(scale * jnp.concatenate([own, other], axis=1))
    return out


def response(force, mixing, diff, gate, damp):
    planes = [force]
    for made in (2, 3):
        planes = linear_step(planes, made, mixing, diff, gate, damp)
        planes[0] = planes[0] + force
    return planes


def turn_kernel(*refs):
    info_ref, mix_ref, coef_ref, top_ref = refs[:4]
    hops, routes_hbm, w_hbm = refs[4:10], refs[10:14], refs[14]
    send_ref, resp_ref = refs[15:17]
    routes, (w, surf, count, sems, work) = refs[17:21], refs[21:]
    fetch_start(routes_hbm, routes, w_hbm, w, sems)
    send_ref[...] = jnp.zeros_like(send_ref)
    diff, gate, damp, _ = coefs(coef_ref)
    mixing = [mix_ref[k] for k in range(3)]
    force = forcing(info_ref, hops, coef_ref, work)
    for f in range(2):
        planes = response(force[f], mixing, diff, gate, damp)
        top = top_ref[f] + planes[0][NEAR : NEAR + CX, 0:LANES]
        surf[pl.ds(f, CX, stride=8), :] = rounded(top)
        for k in range(3):
            resp_ref[3 * f + k] = planes[k]

    def put(group, row, out):
        send_ref[pl.ds(group * 8 + row, 1), :] = out[0:1]
        send_ref[pl.ds(group * 8 + row + 1, 1), :] = out[1:2]

    write_contributions(routes_hbm, routes, w_hbm, w, sems, surf, count, put, None)


def turn(info, mixing, coef, top, hops, routes, weights, columns):
    pairs = weights.shape[0]
    return pl.pallas_call(
        turn_kernel,
        in_specs=[SM, SM] + [VM] * 8 + [HB] * 5,
        out_specs=[VM] * 2,
        out_shape=[struct(columns * 8, LANES), struct(6, TALL, RING)],
        scratch_shapes=pair_scratch(pairs, columns) + [pltpu.VMEM((4 * TALL, LANES), f32)],
        compiler_params=params(),
        name="turn",
    )(info, mixing, coef, top, *hops, *in_hbm(*routes, weights))


def sum_blocks(got_ref, chunk, marks, dense_ref):
    columns = got_ref.shape[0] // chunk
    for part in range(2):
        total = None
        for slot in range(2):
            k = part * 4 + slot * 2
            vals = [got_ref[pl.ds(k + f, columns, stride=chunk), :] for f in range(2)]
            vals = jnp.concatenate(vals, axis=1)
            vals = jnp.concatenate([vals, jnp.zeros((LANES - columns, RING), f32)], axis=0)
            seg = (part * 2 + slot) * CX
            here = exact_dot(marks[seg : seg + CX], vals)
            total = here if total is None else total + here
        for f in range(2):
            dense_ref[pl.ds(part * 2 + f, CX, stride=4), :] = total[:, f * LANES : (f + 1) * LANES]


def first_dense_kernel(got_ref, dense_ref, marks_ref):
    columns = got_ref.shape[0] // 9
    marks = got_ref[pl.ds(8, columns, stride=9), :]
    marks = jnp.concatenate([marks, jnp.zeros((LANES - columns, LANES), f32)], axis=0).T
    marks_ref[...] = marks[0:64]
    sum_blocks(got_ref, 9, marks, dense_ref)


def next_dense_kernel(got_ref, marks_ref, dense_ref):
    sum_blocks(got_ref, 8, marks_ref[...], dense_ref)


def densify(got, marks):
    first = marks is None
    out = struct(64, LANES)
    return pl.pallas_call(
        first_dense_kernel if first else next_dense_kernel,
        in_specs=[VM] if first else [VM, VM],
        out_specs=[VM, VM] if first else VM,
        out_shape=[out, out] if first else out,
        compiler_params=params(),
        name="densify",
    )(*([got] if first else [got, marks]))


def widen(own, other):
    return jnp.concatenate([other[120:128], own, other[0:8]], axis=0)


def bulk_kernel(
    mixrow_ref, mix_ref, cells_ref, coef_ref, resp_ref,
    low_ref, high_ref, side_ref, clow_ref, chigh_ref,
    out_ref, fa, fb, diff, gate, self_, work,
):
    lanes = lax.broadcasted_iota(jnp.int32, (1, LANES), 1)
    level = jnp.where(lanes >= LEV, lanes - LEV, lanes)
    mix = mixrow_ref[...]
    mix_up = jnp.where(level == LEV - 1, 0.0, mix)
    mix_low = jnp.where(level == 0, 0.0, mix)
    mix_mid = -(mix_up + mix_low)

    for x in range(CX):
        fa[HALO + x, 16:144] = cells_ref[x]
        fa[HALO + x, 8:16] = side_ref[16 * x + 8 : 16 * x + 16]
        fa[HALO + x, 144:152] = side_ref[16 * x : 16 * x + 8]
    for j in range(HALO):
        for at, along, corner in ((j, high_ref, chigh_ref), (HALO + CX + j, low_ref, clow_ref)):
            fa[at, 16:144] = along[j * LANES : (j + 1) * LANES]
            fa[at, 8:16] = corner[16 * j + 8 : 16 * j + 16]
            fa[at, 144:152] = corner[16 * j : 16 * j + 8]

    work[...] = jnp.zeros_like(work)

    def columns_of(one, two):
        wide = []
        for part in range(2):
            at = slice(part * LANES, (part + 1) * LANES)
            work[0:TALL] = coef_ref[one * TALL : (one + 1) * TALL, at]
            work[64 : 64 + TALL] = coef_ref[two * TALL : (two + 1) * TALL, at]
            wide.append(work[...].T)
        return widen(*wide)

    both = columns_of(0, 1)
    damping = columns_of(2, 2)
    for i in range(CX + 2 * HALO - 2):
        at = i + NEAR - HALO + 1
        d = jnp.broadcast_to(both[:, at : at + 1], (WIDE, LANES))
        g = jnp.broadcast_to(both[:, 64 + at : 65 + at], (WIDE, LANES))
        damp = jnp.where(level == 0, pltpu.roll(damping, LANES - at, 1), 0.0)
        diff[i] = d
        gate[i] = g
        self_[i] = (1.0 - 4.0 * d) + (g * mix_mid - damp)

    def advance(src, dst, x):
        for y in range(8, 8 + WIDE, CHUNK):
            at = slice(y, y + CHUNK)
            k = slice(y - 8, y - 8 + CHUNK)
            c = src[x, at]
            near = (src[x - 1, at] + src[x + 1, at]) + (
                src[x, y - 1 : y - 1 + CHUNK] + src[x, y + 1 : y + 1 + CHUNK]
            )
            vert = mix_up * pltpu.roll(c, LANES - 1, 1) + mix_low * pltpu.roll(c, 1, 1)
            dst[x, at] = self_[x - 1, k] * c + diff[x - 1, k] * near + gate[x - 1, k] * vert

    src, dst = fa, fb
    for step in range(1, HALO + 1):

        def body(x, carry, src=src, dst=dst):
            advance(src, dst, x)
            return carry

        lax.fori_loop(step, CX + 2 * HALO - step, body, 0, unroll=True)
        src, dst = dst, src
    for x in range(CX):
        out_ref[pl.ds(x, LANES, stride=CX), :] = src[HALO + x, 16:144].T

    d, g, c, _ = coefs(coef_ref)
    mixing = [mix_ref[k] for k in range(6)]
    for f in range(2):
        planes = [resp_ref[3 * f + k] for k in range(3)]
        for made in (4, 5, 6):
            planes = linear_step(planes, made, mixing, d, g, c)
        for k in range(6):
            at = (f * LEV + k) * CX
            out_ref[at : at + CX] += planes[k][NEAR : NEAR + CX, 0:LANES]


def bulk(mixrow, mixing, cells, coef, resp, halo):
    big = pltpu.VMEM((CX + 2 * HALO, WIDE + 16, LANES), f32)
    coefficient = pltpu.VMEM((CX + 2 * HALO - 2, WIDE, LANES), f32)
    return pl.pallas_call(
        bulk_kernel,
        in_specs=[VM, SM] + [VM] * 8,
        out_specs=VM,
        out_shape=struct(2 * LEV * CX, LANES),
        scratch_shapes=[big, big] + [coefficient] * 3 + [pltpu.VMEM((LANES, LANES), f32)],
        compiler_params=params(),
        cost_estimate=pl.CostEstimate(flops=40_000_000, transcendentals=0, bytes_accessed=40_000_000),
        name="bulk",
    )(mixrow, mixing, cells, coef, resp, *halo)


def final_kernel(info_ref, mix_ref, coef_ref, a, b, l1, l2, h1, h2, part_ref, out_ref, work):
    diff, gate, damp, _ = coefs(coef_ref)
    mixing = [mix_ref[k] for k in range(3)]
    force = forcing(info_ref, (a, b, l1, l2, h1, h2), coef_ref, work)
    for f in range(2):
        planes = response(force[f], mixing, diff, gate, damp)
        for k in range(3):
            out_ref[f, k] = part_ref[f, k] + planes[k][NEAR : NEAR + CX, 0:LANES]


def final(info, mixing, coef, hops, part):
    block = pl.BlockSpec((2, 3, CX, LANES), lambda i: (0, 0, 0, 0))
    return pl.pallas_call(
        final_kernel,
        grid=(1,),
        in_specs=[SM, SM] + [VM] * 7 + [block],
        out_specs=block,
        out_shape=struct(2, LEV, CX, LANES),
        input_output_aliases={9: 0},
        scratch_shapes=[pltpu.VMEM((4 * TALL, LANES), f32)],
        compiler_params=params(),
        name="final",
    )(info, mixing, coef, *hops, part)


def solution(mesh):
    comps, columns, halves = (mesh.shape[a] for a in AXES)

    def sent(value, where):
        pairs = []
        for s in range(comps):
            for g in range(columns):
                for h in range(halves):
                    a, b, c = where(s, g, h)
                    b, c = b % columns, c % halves
                    pairs.append(((s * columns + g) * halves + h, (a * columns + b) * halves + c))
        return lax.ppermute(value, AXES, pairs)

    def exchanged(low, high, side, clow, chigh):
        return (
            sent(low, lambda s, g, h: (s, g - 1, h)),
            sent(high, lambda s, g, h: (s, g + 1, h)),
            sent(side, lambda s, g, h: (s, g, h + 1)),
            sent(clow, lambda s, g, h: (s, g - 1, h + 1)),
            sent(chigh, lambda s, g, h: (s, g + 1, h + 1)),
        )

    def hopped(dense):
        first, final_ = dense[: 4 * NEAR], dense[4 * (CX - NEAR) :]
        return (
            sent(dense, lambda s, g, h: (1 - s, g, h)),
            sent(dense, lambda s, g, h: (1 - s, g, h + 1)),
            sent(final_, lambda s, g, h: (1 - s, g + 1, h)),
            sent(final_, lambda s, g, h: (1 - s, g + 1, h + 1)),
            sent(first, lambda s, g, h: (1 - s, g - 1, h)),
            sent(first, lambda s, g, h: (1 - s, g - 1, h + 1)),
        )

    def body(
        state, diffusion, vertical, coupling, land_sea,
        route_tile, route_src, route_dst, pair_cols, intersection,
    ):
        info = jnp.stack([lax.axis_index("comp"), lax.axis_index("gy")]).astype(jnp.int32)
        mixing = vertical[0]
        mixrow = jnp.concatenate([vertical, vertical], axis=1)
        routes = (route_tile[0, 0, :, 0], route_src[0, 0], route_dst[0, 0], pair_cols[0, 0])
        weights = intersection[0, 0]

        send = first_contributions(routes, weights, state[0], columns)
        got = lax.all_to_all(send, "gx", 0, 0, tiled=True)
        cells, nat, *edges = prepare(
            info, state.reshape(-1, LANES), diffusion[0], coupling[0], land_sea[0]
        )
        halo = exchanged(*edges)
        coef, top = gather(mixing, nat, halo)
        dense, marks = densify(got.reshape(-1, LANES), None)
        hops = hopped(dense)
        send, resp = turn(info, mixing, coef, top, hops, routes, weights, columns)

        got = lax.all_to_all(send, "gx", 0, 0, tiled=True)
        part = bulk(mixrow, mixing, cells, coef, resp, halo)
        got, part = lax.optimization_barrier((got, part))
        hops = hopped(densify(got, marks))
        out = final(info, mixing, coef, hops, part.reshape(state.shape[1:]))
        return out[None]

    spec = P("comp", "gx", "gy")
    route = P("comp", ("gx", "gy"))
    return jax.shard_map(
        body,
        mesh=mesh,
        in_specs=(
            P("comp", None, None, "gx", "gy"), spec, P("comp", None), spec, spec,
            route, route, route, route, route,
        ),
        out_specs=P("comp", None, None, "gx", "gy"),
        check_vma=False,
    )
```

profile of v0, /device:TPU:6, one launch (start us, length us, event | category | flops | bytes accessed | tf_op | source)
XLA Modules:
  0.0 96.3 jit_solution(8641847324143620052)
XLA Ops:
  0.0 0.0 copy-start
  0.0 0.0 copy-start.3
  0.0 0.0 copy-start.2
  0.0 0.0 copy-start.1
  0.0 0.0 copy-start.4
  0.0 4.5 %contrib.1 = f32[576,1,128]{2,1,0:T(1,128)} custom-call(s32[64]{0:T(128)} %bitcast.32, s32[64]{0:T(128)} %bitcast.34, s32[64]{0:T(128)} %bitcast.36, s32[64]{0:T(128)} %bitcast.38, bf16[64,128,128]{2,1,0:T(8,128)(2,1)} %bitcast.29, f32[2,64,16,128]{3,2,1,0:T(8,128)} %bitcast.18), custom_call_target="tpu_custom_call" | custom-call | tf_op jit(solution)/shard_map/contrib/pallas_call | solution.py:128
  4.5 12.1 %all-to-all-start = ((f32[576,1,128]{2,1,0:T(1,128)}), f32[576,1,128]{2,1,0:T(1,128)S(1)}, u32[]{:S(2)}, u32[]{:S(2)}) async-start(f32[576,1,128]{2,1,0:T(1,128)} %contrib.1), calls=%async_computation | async-start | bytes 589824 | tf_op jit(solution)/shard_map/all_to_all | solution.py:532
  16.6 0.1 pad_add_fusion.info_ref.refs_0_
  16.7 0.0 copy-done
  16.7 0.0 copy-done.3
  16.7 0.0 copy-done.2
  16.7 0.0 copy-done.1
  16.7 1.8 %prepare.1 = (f32[16,128,128]{2,1,0:T(8,128)S(1)}, f32[192,128]{1,0:T(8,128)S(1)}, f32[864,128]{1,0:T(8,128)}, f32[864,128]{1,0:T(8,128)S(1)}, f32[448,128]{1,0:...) custom-call(s32[2]{0:T(128)S(1)} %pad_add_fusion.info_ref.refs_0_, f32[2048,128]{1,0:T(8,128)S(1)} %bitcast.19, ...), custom_call_target="tpu_custom_call" | custom-call | tf_op jit(solution)/shard_map/prepare/pallas_call | solution.py:185
  18.5 4.9 %collective-permute-start = (f32[864,128]{1,0:T(8,128)}, f32[864,128]{1,0:T(8,128)S(1)}, u32[]{:S(2)}, u32[]{:S(2)}) collective-permute-start(f32[864,128]{1,0:T(8,128)} %get-tuple-element.21), channel_id=1, source_target_pairs={{0,126},{1,127},{2,0},{3,1},{4,2},{5,3},{6,4},{7,5},{8,6},{9,7},{1... | collective-permute-start | bytes 1327112 | tf_op jit(solution)/shard_map/ppermute | solution.py:499
  23.4 0.0 collective-permute-start.1
  23.4 0.8 collective-permute-start.2
  24.3 5.4 %collective-permute-start.3 = (f32[192,128]{1,0:T(8,128)}, f32[192,128]{1,0:T(8,128)S(1)}, u32[]{:S(2)}, u32[]{:S(2)}) collective-permute-start(f32[192,128]{1,0:T(8,128)} %get-tuple-element.24), channel_id=1, source_target_pairs={{0,127},{1,126},{2,1},{3,0},{4,3},{5,2},{6,5},{7,4},{8,7},{9,6},{1... | collective-permute-start | bytes 294920 | tf_op jit(solution)/shard_map/ppermute | solution.py:499
  29.7 0.0 collective-permute-start.4
  29.7 0.4 all-to-all-done
  30.1 0.3 densify.2
  30.4 1.8 %collective-permute-done.3.clow_ref = f32[192,128]{1,0:T(8,128)S(1)} collective-permute-done((f32[192,128]{1,0:T(8,128)}, f32[192,128]{1,0:T(8,128)S(1)}, u32[]{:S(2)}, u32[]{:S(2)}) %collective-permute-start.3) | collective-permute-done | bytes 98336 | tf_op jit(solution)/shard_map/ppermute | solution.py:499
  32.2 5.9 %collective-permute-start.10 = (f32[32,128]{1,0:T(8,128)S(1)}, f32[32,128]{1,0:T(8,128)S(1)}, u32[]{:S(2)}, u32[]{:S(2)}) collective-permute-start(f32[32,128]{1,0:T(8,128)S(1)} %get-tuple-element.37), channel_id=1, source_target_pairs={{0,255},{1,254},{2,129},{3,128},{4,131},{5,130},{6,133},{7,132},{8... | collective-permute-start | bytes 49160 | tf_op jit(solution)/shard_map/ppermute | solution.py:499
  38.1 0.0 collective-permute-done.4.chigh_ref
  38.1 2.1 %collective-permute-start.6 = (f32[64,128]{1,0:T(8,128)S(1)}, f32[64,128]{1,0:T(8,128)S(1)}, u32[]{:S(2)}, u32[]{:S(2)}) collective-permute-start(f32[64,128]{1,0:T(8,128)S(1)} %get-tuple-element.28), channel_id=1, source_target_pairs={{0,129},{1,128},{2,131},{3,130},{4,133},{5,132},{6,135},{7,134},{8... | collective-permute-start | bytes 98312 | tf_op jit(solution)/shard_map/ppermute | solution.py:499
  40.2 0.0 collective-permute-done.2.side_ref
  40.2 0.6 collective-permute-start.5
  40.9 0.0 collective-permute-done.low_ref
  40.9 1.8 %collective-permute-start.9 = (f32[32,128]{1,0:T(8,128)S(1)}, f32[32,128]{1,0:T(8,128)S(1)}, u32[]{:S(2)}, u32[]{:S(2)}) collective-permute-start(f32[32,128]{1,0:T(8,128)S(1)} %get-tuple-element.37), channel_id=1, source_target_pairs={{0,254},{1,255},{2,128},{3,129},{4,130},{5,131},{6,132},{7,133},{8... | collective-permute-start | bytes 49160 | tf_op jit(solution)/shard_map/ppermute | solution.py:499
  42.7 0.0 collective-permute-done.1.high_ref
  42.7 1.9 %collective-permute-start.8 = (f32[32,128]{1,0:T(8,128)S(1)}, f32[32,128]{1,0:T(8,128)S(1)}, u32[]{:S(2)}, u32[]{:S(2)}) collective-permute-start(f32[32,128]{1,0:T(8,128)S(1)} %get-tuple-element.38), channel_id=1, source_target_pairs={{0,131},{1,130},{2,133},{3,132},{4,135},{5,134},{6,137},{7,136},{8... | collective-permute-start | bytes 49160 | tf_op jit(solution)/shard_map/ppermute | solution.py:499
  44.6 0.0 collective-permute-done.10.refs_9_
  44.6 0.0 collective-permute-start.7
  44.6 0.0 copy-done.4
  44.6 0.8 gather.1
  45.4 0.3 collective-permute-done.9.refs_8_
  45.7 5.6 %collective-permute-done.8.refs_7_ = f32[32,128]{1,0:T(8,128)S(1)} collective-permute-done((f32[32,128]{1,0:T(8,128)S(1)}, f32[32,128]{1,0:T(8,128)S(1)}, u32[]{:S(2)}, u32[]{:S(2)}) %collective-permute-start.8) | collective-permute-done | bytes 16416 | tf_op jit(solution)/shard_map/ppermute | solution.py:499
  51.3 2.2 %collective-permute-done.7.refs_6_ = f32[32,128]{1,0:T(8,128)S(1)} collective-permute-done((f32[32,128]{1,0:T(8,128)S(1)}, f32[32,128]{1,0:T(8,128)S(1)}, u32[]{:S(2)}, u32[]{:S(2)}) %collective-permute-start.7) | collective-permute-done | bytes 16416 | tf_op jit(solution)/shard_map/ppermute | solution.py:499
  53.5 0.0 collective-permute-done.6.refs_5_
  53.5 0.0 collective-permute-done.5.refs_4_
  53.5 4.3 %turn.1 = (f32[512,128]{1,0:T(8,128)}, f32[6,32,256]{2,1,0:T(8,128)S(1)}) custom-call(s32[2]{0:T(128)S(1)} %pad_add_fusion.info_ref.refs_0_, f32[64]{0:T(128)S(1)} %bitcast.26, f32[128,256]{1,0:T(8,128)S(1)} %get-tuple-element.26.refs_2_.coef_ref, f32[2,16,128]{2,1,0:T(8,128)S(1)} %get-tuple-element.27.refs_3_, ...), custom_call_target="tpu_custom_call" | custom-call | tf_op jit(solution)/shard_map/turn/pallas_call | solution.py:314
  57.8 5.3 %all-to-all-start.1 = ((f32[64,8,128]{2,1,0:T(8,128)}), f32[64,8,128]{2,1,0:T(8,128)S(1)}, u32[]{:S(2)}, u32[]{:S(2)}) async-start(f32[64,8,128]{2,1,0:T(8,128)} %bitcast.14), calls=%async_computation.1 | async-start | bytes 524288 | tf_op jit(solution)/shard_map/all_to_all | solution.py:542
  63.2 0.1 pad_maximum_fusion.mixrow_ref
  63.2 9.1 %bulk.1 = f32[2048,128]{1,0:T(8,128)} custom-call(f32[1,128]{1,0:T(1,128)S(1)} %pad_maximum_fusion.mixrow_ref, f32[64]{0:T(128)S(1)} %bitcast.27, f32[16,128,128]{2,1,0:T(8,128)S(1)} %get-tuple-element.30.cells_ref, f32[128,256]{1,0:T(8,128)S(1)} %get-tuple-element.26.refs_2_.coef_ref, f32[6,32,256]{2,1,0:T(8,128)S(1)} %get-tuple-element.31.resp_ref, ...), custom_call_target="tpu_custom_call" | custom-call | flops 40000000 | bytes 40000000 | tf_op jit(solution)/shard_map/bulk/pallas_call | solution.py:451
  72.3 3.8 %all-to-all-done.1 = f32[64,8,128]{2,1,0:T(8,128)S(1)} async-done(((f32[64,8,128]{2,1,0:T(8,128)}), f32[64,8,128]{2,1,0:T(8,128)S(1)}, u32[]{:S(2)}, u32[]{:S(2)}) %all-to-all-start.1) | async-done | bytes 262176 | tf_op jit(solution)/shard_map/all_to_all | solution.py:542
  76.1 0.2 densify.3
  76.4 3.0 %collective-permute-start.16 = (f32[32,128]{1,0:T(8,128)S(1)}, f32[32,128]{1,0:T(8,128)S(1)}, u32[]{:S(2)}, u32[]{:S(2)}) collective-permute-start(f32[32,128]{1,0:T(8,128)S(1)} %get-tuple-element.35), channel_id=1, source_target_pairs={{0,255},{1,254},{2,129},{3,128},{4,131},{5,130},{6,133},{7,132},{8... | collective-permute-start | bytes 49160 | tf_op jit(solution)/shard_map/ppermute | solution.py:499
  79.3 1.1 %collective-permute-start.12 = (f32[64,128]{1,0:T(8,128)S(1)}, f32[64,128]{1,0:T(8,128)S(1)}, u32[]{:S(2)}, u32[]{:S(2)}) collective-permute-start(f32[64,128]{1,0:T(8,128)S(1)} %densify.3), channel_id=1, source_target_pairs={{0,129},{1,128},{2,131},{3,130},{4,133},{5,132},{6,135},{7,134},{8... | collective-permute-start | bytes 98312 | tf_op jit(solution)/shard_map/ppermute | solution.py:499
  80.5 0.0 collective-permute-start.11
  80.5 2.8 %collective-permute-start.15 = (f32[32,128]{1,0:T(8,128)S(1)}, f32[32,128]{1,0:T(8,128)S(1)}, u32[]{:S(2)}, u32[]{:S(2)}) collective-permute-start(f32[32,128]{1,0:T(8,128)S(1)} %get-tuple-element.35), channel_id=1, source_target_pairs={{0,254},{1,255},{2,128},{3,129},{4,130},{5,131},{6,132},{7,133},{8... | collective-permute-start | bytes 49160 | tf_op jit(solution)/shard_map/ppermute | solution.py:499
  83.3 2.6 %collective-permute-start.14 = (f32[32,128]{1,0:T(8,128)S(1)}, f32[32,128]{1,0:T(8,128)S(1)}, u32[]{:S(2)}, u32[]{:S(2)}) collective-permute-start(f32[32,128]{1,0:T(8,128)S(1)} %get-tuple-element.36), channel_id=1, source_target_pairs={{0,131},{1,130},{2,133},{3,132},{4,135},{5,134},{6,137},{7,136},{8... | collective-permute-start | bytes 49160 | tf_op jit(solution)/shard_map/ppermute | solution.py:499
  85.8 0.0 collective-permute-done.16.h2
  85.8 0.0 collective-permute-start.13
  85.8 0.0 collective-permute-done.15.h1
  85.8 6.0 %collective-permute-done.14.l2 = f32[32,128]{1,0:T(8,128)S(1)} collective-permute-done((f32[32,128]{1,0:T(8,128)S(1)}, f32[32,128]{1,0:T(8,128)S(1)}, u32[]{:S(2)}, u32[]{:S(2)}) %collective-permute-start.14) | collective-permute-done | bytes 16416 | tf_op jit(solution)/shard_map/ppermute | solution.py:499
  91.9 2.9 %collective-permute-done.13.l1 = f32[32,128]{1,0:T(8,128)S(1)} collective-permute-done((f32[32,128]{1,0:T(8,128)S(1)}, f32[32,128]{1,0:T(8,128)S(1)}, u32[]{:S(2)}, u32[]{:S(2)}) %collective-permute-start.13) | collective-permute-done | bytes 16416 | tf_op jit(solution)/shard_map/ppermute | solution.py:499
  94.7 0.0 collective-permute-done.12.b
  94.7 0.0 collective-permute-done.11.a
  94.7 1.6 %final.1 = f32[2,64,16,128]{3,2,1,0:T(8,128)} custom-call(s32[2]{0:T(128)S(1)} %pad_add_fusion.info_ref.refs_0_, f32[64]{0:T(128)S(1)} %bitcast.28, f32[128,256]{1,0:T(8,128)S(1)} %get-tuple-element.26.refs_2_.coef_ref, f32[64,128]{1,0:T(8,128)S(1)} %collective-permute-done.11.a, ...), custom_call_target="tpu_custom_call", output_to_operand_aliasing={{}: (9, {})} | custom-call | tf_op jit(solution)/shard_map/final/pallas_call | solution.py:475
  (2 shorter events, 0.0 us)
Async XLA Ops:
  0.0 16.7 %copy-start = (f32[1,2,64,16,128]{4,3,2,1,0:T(8,128)S(1)}, f32[1,2,64,16,128]{4,3,2,1,0:T(8,128)}, u32[]{:S(2)}) copy-start(f32[1,2,64,16,128]{4,3,2,1,0:T(8,128)} %param.10) | copy-start | bytes 3145732
  0.0 16.7 %copy-start.3 = (s32[1,16,128]{2,1,0:T(8,128)S(1)}, s32[1,16,128]{2,1,0:T(8,128)}, u32[]{:S(2)}) copy-start(s32[1,16,128]{2,1,0:T(8,128)} %param.14) | copy-start | bytes 24580
  0.0 16.7 %copy-start.2 = (f32[1,16,128]{2,1,0:T(8,128)S(1)}, f32[1,16,128]{2,1,0:T(8,128)}, u32[]{:S(2)}) copy-start(f32[1,16,128]{2,1,0:T(8,128)} %param.13) | copy-start | bytes 24580
  0.0 16.7 %copy-start.1 = (f32[1,16,128]{2,1,0:T(8,128)S(1)}, f32[1,16,128]{2,1,0:T(8,128)}, u32[]{:S(2)}) copy-start(f32[1,16,128]{2,1,0:T(8,128)} %param.11) | copy-start | bytes 24580
  0.0 44.6 %copy-start.4 = (f32[1,64]{1,0:T(1,128)S(1)}, f32[1,64]{1,0:T(1,128)}, u32[]{:S(2)}) copy-start(f32[1,64]{1,0:T(1,128)} %param.12) | copy-start | bytes 772
  4.5 25.6 %all-to-all-start = ((f32[576,1,128]{2,1,0:T(1,128)}), f32[576,1,128]{2,1,0:T(1,128)S(1)}, u32[]{:S(2)}, u32[]{:S(2)}) async-start(f32[576,1,128]{2,1,0:T(1,128)} %contrib.1), calls=%async_computation | async-start | bytes 589824 | tf_op jit(solution)/shard_map/all_to_all | solution.py:532
  18.5 22.4 %collective-permute-start = (f32[864,128]{1,0:T(8,128)}, f32[864,128]{1,0:T(8,128)S(1)}, u32[]{:S(2)}, u32[]{:S(2)}) collective-permute-start(f32[864,128]{1,0:T(8,128)} %get-tuple-element.21), channel_id=1, source_target_pairs={{0,126},{1,127},{2,0},{3,1},{4,2},{5,3},{6,4},{7,5},{8,6},{9,7},{1... | collective-permute-start | bytes 1327112 | tf_op jit(solution)/shard_map/ppermute | solution.py:499
  23.4 19.3 %collective-permute-start.1 = (f32[864,128]{1,0:T(8,128)S(1)}, f32[864,128]{1,0:T(8,128)S(1)}, u32[]{:S(2)}, u32[]{:S(2)}) collective-permute-start(f32[864,128]{1,0:T(8,128)S(1)} %get-tuple-element.22), channel_id=1, source_target_pairs={{0,2},{1,3},{2,4},{3,5},{4,6},{5,7},{6,8},{7,9},{8,10},{9,11},{10,... | collective-permute-start | bytes 1327112 | tf_op jit(solution)/shard_map/ppermute | solution.py:499
  23.4 16.8 %collective-permute-start.2 = (f32[448,128]{1,0:T(8,128)}, f32[448,128]{1,0:T(8,128)S(1)}, u32[]{:S(2)}, u32[]{:S(2)}) collective-permute-start(f32[448,128]{1,0:T(8,128)} %get-tuple-element.23), channel_id=1, source_target_pairs={{0,1},{1,0},{2,3},{3,2},{4,5},{5,4},{6,7},{7,6},{8,9},{9,8},{10,11... | collective-permute-start | bytes 688136 | tf_op jit(solution)/shard_map/ppermute | solution.py:499
  24.3 7.9 %collective-permute-start.3 = (f32[192,128]{1,0:T(8,128)}, f32[192,128]{1,0:T(8,128)S(1)}, u32[]{:S(2)}, u32[]{:S(2)}) collective-permute-start(f32[192,128]{1,0:T(8,128)} %get-tuple-element.24), channel_id=1, source_target_pairs={{0,127},{1,126},{2,1},{3,0},{4,3},{5,2},{6,5},{7,4},{8,7},{9,6},{1... | collective-permute-start | bytes 294920 | tf_op jit(solution)/shard_map/ppermute | solution.py:499
  29.7 8.4 %collective-permute-start.4 = (f32[192,128]{1,0:T(8,128)S(1)}, f32[192,128]{1,0:T(8,128)S(1)}, u32[]{:S(2)}, u32[]{:S(2)}) collective-permute-start(f32[192,128]{1,0:T(8,128)S(1)} %get-tuple-element.25), channel_id=1, source_target_pairs={{0,3},{1,2},{2,5},{3,4},{4,7},{5,6},{6,9},{7,8},{8,11},{9,10},{10,... | collective-permute-start | bytes 294920 | tf_op jit(solution)/shard_map/ppermute | solution.py:499
  32.2 12.4 %collective-permute-start.10 = (f32[32,128]{1,0:T(8,128)S(1)}, f32[32,128]{1,0:T(8,128)S(1)}, u32[]{:S(2)}, u32[]{:S(2)}) collective-permute-start(f32[32,128]{1,0:T(8,128)S(1)} %get-tuple-element.37), channel_id=1, source_target_pairs={{0,255},{1,254},{2,129},{3,128},{4,131},{5,130},{6,133},{7,132},{8... | collective-permute-start | bytes 49160 | tf_op jit(solution)/shard_map/ppermute | solution.py:499
  38.1 15.4 %collective-permute-start.6 = (f32[64,128]{1,0:T(8,128)S(1)}, f32[64,128]{1,0:T(8,128)S(1)}, u32[]{:S(2)}, u32[]{:S(2)}) collective-permute-start(f32[64,128]{1,0:T(8,128)S(1)} %get-tuple-element.28), channel_id=1, source_target_pairs={{0,129},{1,128},{2,131},{3,130},{4,133},{5,132},{6,135},{7,134},{8... | collective-permute-start | bytes 98312 | tf_op jit(solution)/shard_map/ppermute | solution.py:499
  40.2 13.3 %collective-permute-start.5 = (f32[64,128]{1,0:T(8,128)S(1)}, f32[64,128]{1,0:T(8,128)S(1)}, u32[]{:S(2)}, u32[]{:S(2)}) collective-permute-start(f32[64,128]{1,0:T(8,128)S(1)} %get-tuple-element.28), channel_id=1, source_target_pairs={{0,128},{1,129},{2,130},{3,131},{4,132},{5,133},{6,134},{7,135},{8... | collective-permute-start | bytes 98312 | tf_op jit(solution)/shard_map/ppermute | solution.py:499
  40.9 4.8 %collective-permute-start.9 = (f32[32,128]{1,0:T(8,128)S(1)}, f32[32,128]{1,0:T(8,128)S(1)}, u32[]{:S(2)}, u32[]{:S(2)}) collective-permute-start(f32[32,128]{1,0:T(8,128)S(1)} %get-tuple-element.37), channel_id=1, source_target_pairs={{0,254},{1,255},{2,128},{3,129},{4,130},{5,131},{6,132},{7,133},{8... | collective-permute-start | bytes 49160 | tf_op jit(solution)/shard_map/ppermute | solution.py:499
  42.7 8.6 %collective-permute-start.8 = (f32[32,128]{1,0:T(8,128)S(1)}, f32[32,128]{1,0:T(8,128)S(1)}, u32[]{:S(2)}, u32[]{:S(2)}) collective-permute-start(f32[32,128]{1,0:T(8,128)S(1)} %get-tuple-element.38), channel_id=1, source_target_pairs={{0,131},{1,130},{2,133},{3,132},{4,135},{5,134},{6,137},{7,136},{8... | collective-permute-start | bytes 49160 | tf_op jit(solution)/shard_map/ppermute | solution.py:499
  44.6 8.9 %collective-permute-start.7 = (f32[32,128]{1,0:T(8,128)S(1)}, f32[32,128]{1,0:T(8,128)S(1)}, u32[]{:S(2)}, u32[]{:S(2)}) collective-permute-start(f32[32,128]{1,0:T(8,128)S(1)} %get-tuple-element.38), channel_id=1, source_target_pairs={{0,130},{1,131},{2,132},{3,133},{4,134},{5,135},{6,136},{7,137},{8... | collective-permute-start | bytes 49160 | tf_op jit(solution)/shard_map/ppermute | solution.py:499
  57.8 18.3 %all-to-all-start.1 = ((f32[64,8,128]{2,1,0:T(8,128)}), f32[64,8,128]{2,1,0:T(8,128)S(1)}, u32[]{:S(2)}, u32[]{:S(2)}) async-start(f32[64,8,128]{2,1,0:T(8,128)} %bitcast.14), calls=%async_computation.1 | async-start | bytes 524288 | tf_op jit(solution)/shard_map/all_to_all | solution.py:542
  76.4 9.4 %collective-permute-start.16 = (f32[32,128]{1,0:T(8,128)S(1)}, f32[32,128]{1,0:T(8,128)S(1)}, u32[]{:S(2)}, u32[]{:S(2)}) collective-permute-start(f32[32,128]{1,0:T(8,128)S(1)} %get-tuple-element.35), channel_id=1, source_target_pairs={{0,255},{1,254},{2,129},{3,128},{4,131},{5,130},{6,133},{7,132},{8... | collective-permute-start | bytes 49160 | tf_op jit(solution)/shard_map/ppermute | solution.py:499
  79.3 15.4 %collective-permute-start.12 = (f32[64,128]{1,0:T(8,128)S(1)}, f32[64,128]{1,0:T(8,128)S(1)}, u32[]{:S(2)}, u32[]{:S(2)}) collective-permute-start(f32[64,128]{1,0:T(8,128)S(1)} %densify.3), channel_id=1, source_target_pairs={{0,129},{1,128},{2,131},{3,130},{4,133},{5,132},{6,135},{7,134},{8... | collective-permute-start | bytes 98312 | tf_op jit(solution)/shard_map/ppermute | solution.py:499
  80.5 14.2 %collective-permute-start.11 = (f32[64,128]{1,0:T(8,128)S(1)}, f32[64,128]{1,0:T(8,128)S(1)}, u32[]{:S(2)}, u32[]{:S(2)}) collective-permute-start(f32[64,128]{1,0:T(8,128)S(1)} %densify.3), channel_id=1, source_target_pairs={{0,128},{1,129},{2,130},{3,131},{4,132},{5,133},{6,134},{7,135},{8... | collective-permute-start | bytes 98312 | tf_op jit(solution)/shard_map/ppermute | solution.py:499
  80.5 5.4 %collective-permute-start.15 = (f32[32,128]{1,0:T(8,128)S(1)}, f32[32,128]{1,0:T(8,128)S(1)}, u32[]{:S(2)}, u32[]{:S(2)}) collective-permute-start(f32[32,128]{1,0:T(8,128)S(1)} %get-tuple-element.35), channel_id=1, source_target_pairs={{0,254},{1,255},{2,128},{3,129},{4,130},{5,131},{6,132},{7,133},{8... | collective-permute-start | bytes 49160 | tf_op jit(solution)/shard_map/ppermute | solution.py:499
  83.3 8.6 %collective-permute-start.14 = (f32[32,128]{1,0:T(8,128)S(1)}, f32[32,128]{1,0:T(8,128)S(1)}, u32[]{:S(2)}, u32[]{:S(2)}) collective-permute-start(f32[32,128]{1,0:T(8,128)S(1)} %get-tuple-element.36), channel_id=1, source_target_pairs={{0,131},{1,130},{2,133},{3,132},{4,135},{5,134},{6,137},{7,136},{8... | collective-permute-start | bytes 49160 | tf_op jit(solution)/shard_map/ppermute | solution.py:499
  85.8 8.9 %collective-permute-start.13 = (f32[32,128]{1,0:T(8,128)S(1)}, f32[32,128]{1,0:T(8,128)S(1)}, u32[]{:S(2)}, u32[]{:S(2)}) collective-permute-start(f32[32,128]{1,0:T(8,128)S(1)} %get-tuple-element.36), channel_id=1, source_target_pairs={{0,130},{1,131},{2,132},{3,133},{4,134},{5,135},{6,136},{7,137},{8... | collective-permute-start | bytes 49160 | tf_op jit(solution)/shard_map/ppermute | solution.py:499
where the time goes:
time: 96.6 us; the launch traced here: 96.3 us
  starting transfers between devices  50.5 us (52%)
  waiting for transfers between devices  23 us (24%)
  Pallas kernels  22.6 us (23%)
    ppermute x17, starting transfers between devices, sent(): return lax.ppermute(value, AXES, pairs)  33 us
    ppermute x17, waiting for transfers between devices, sent(): return lax.ppermute(value, AXES, pairs)  18.8 us
    all_to_all x2, starting transfers between devices, body(): got = lax.all_to_all(send, 'gx', 0, 0, tiled=True)  17.5 us
    pallas_call x1, Pallas kernels, bulk(): pl.pallas_call(bulk_kernel, in_specs=[VM, SM] + [VM] * 8, out_specs=VM, o...  9.06 us
    pallas_call x1, Pallas kernels, first_contributions(): pl.pallas_call(first_kernel, in_specs=[HB] * 6, out_specs=VM, out_shape=s...  4.47 us
    pallas_call x1, Pallas kernels, turn(): pl.pallas_call(turn_kernel, in_specs=[SM, SM] + [VM] * 8 + [HB] * 5, out_...  4.3 us
    all_to_all x2, waiting for transfers between devices, body(): got = lax.all_to_all(send, 'gx', 0, 0, tiled=True)  4.21 us
  transfers between devices with their start and end apart: 19, of which 8 were waited for; matrix products, arithmetic and copies ran while one was open for 0% of the time, Pallas kernels for 12%

commit v1 on v0

--- a/solution.py
+++ b/solution.py
@@ -56,14 +56,10 @@
 
 def write_contributions(routes_hbm, routes, w_hbm, w, sems, surf, count, put, mark):
     tile_ref, src_ref, dst_ref, cols_ref = routes
+    for i in range(count.shape[0]):
+        count[i] = 0
     for i in range(4):
         pltpu.make_async_copy(routes_hbm[i], routes[i], sems.at[i]).wait()
-
-    def clear(i, c):
-        count[i] = 0
-        return c
-
-    lax.fori_loop(0, count.shape[0], clear, 0)
     lanes = lax.broadcasted_iota(jnp.int32, (1, LANES), 1)
     per = w.shape[0] // PARTS
     for p in range(w.shape[0]):
@@ -137,10 +133,29 @@
     )(*in_hbm(*routes, weights, state))
 
 
+EDGE = HALO * LANES
+EDGE_NAT = EDGE + NAT * NEAR
+EDGE_ROWS = EDGE_NAT + NAT * NEAR + HALO * 16
+SIDE = NAT * NEAR
+SIDE_NAT = SIDE + 16 * CX
+SIDE_ROWS = SIDE_NAT + NAT * NEAR
+CORNER = NAT * NEAR + HALO * 16
+
+
 def prepare_kernel(
-    info_ref, state_ref, diff_ref, coup_ref, sea_ref,
-    cells_ref, nat_ref, low_ref, high_ref, side_ref, clow_ref, chigh_ref,
+    info_ref, state_hbm, diff_hbm, coup_hbm, sea_hbm, cells_ref, nat_ref, side_ref,
+    state_ref, diff_ref, coup_ref, sea_ref, sems,
 ):
+    copies = [
+        pltpu.make_async_copy(a, b, sems.at[i])
+        for i, (a, b) in enumerate(
+            ((diff_hbm, diff_ref), (coup_hbm, coup_ref), (sea_hbm, sea_ref), (state_hbm, state_ref))
+        )
+    ]
+    for copy in copies:
+        copy.start()
+    for copy in copies[:3]:
+        copy.wait()
     sea = sea_ref[...].astype(f32)
     gate = jnp.where(info_ref[0] == 1, sea, jnp.ones_like(sea))
     coup = gate * coup_ref[...]
@@ -148,51 +163,60 @@
     nat_ref[16:32] = gate
     nat_ref[32:48] = coup
     nat_ref[48:64] = coup * sea
+    copies[3].wait()
     for f in range(2):
         nat_ref[64 * (f + 1) : 64 * (f + 2)] = state_ref[f * LEV * CX : f * LEV * CX + 64]
+    for k in range(NAT):
+        at = k * NEAR
+        side_ref[at : at + NEAR] = nat_ref[k * CX : k * CX + NEAR]
+        side_ref[SIDE_NAT + at : SIDE_NAT + at + NEAR] = nat_ref[(k + 1) * CX - NEAR : (k + 1) * CX]
     for x in range(CX):
         row = state_ref[pl.ds(x, LANES, stride=CX), :].T
         cells_ref[x] = row
-        for j, piece in enumerate((row[0:8], row[120:128])):
-            at = 16 * x + 8 * j
-            side_ref[at : at + 8] = piece
-            if x < HALO:
-                clow_ref[at : at + 8] = piece
-            if x >= CX - HALO:
-                at -= 16 * (CX - HALO)
-                chigh_ref[at : at + 8] = piece
-        if x < HALO:
-            low_ref[x * LANES : (x + 1) * LANES] = row
-        if x >= CX - HALO:
-            at = x - (CX - HALO)
-            high_ref[at * LANES : (at + 1) * LANES] = row
-    side_ref[16 * CX :] = nat_ref[...]
+        at = SIDE + 16 * x
+        side_ref[at : at + 8] = row[0:8]
+        side_ref[at + 8 : at + 16] = row[120:128]
+
+
+def prepare(info, state, diffusion, coupling, land_sea):
+    tile = pltpu.VMEM((CX, LANES), f32)
+    return pl.pallas_call(
+        prepare_kernel,
+        in_specs=[SM] + [HB] * 4,
+        out_specs=[VM] * 3,
+        out_shape=[
+            struct(CX, LANES, LANES), struct(NAT * CX, LANES), struct(SIDE_ROWS, LANES),
+        ],
+        scratch_shapes=[
+            pltpu.VMEM(state.shape, f32), tile, tile, pltpu.VMEM((CX, LANES), jnp.int32),
+            pltpu.SemaphoreType.DMA((4,)),
+        ],
+        compiler_params=params(),
+        name="prepare",
+    )(info, *in_hbm(state, diffusion, coupling, land_sea))
+
+
+def pack_kernel(cells_ref, nat_ref, side_ref, low_ref, high_ref):
+    for j in range(HALO):
+        low_ref[j * LANES : (j + 1) * LANES] = cells_ref[j]
+        high_ref[j * LANES : (j + 1) * LANES] = cells_ref[CX - HALO + j]
     for k in range(NAT):
-        first = nat_ref[k * CX : k * CX + NEAR]
-        final = nat_ref[(k + 1) * CX - NEAR : (k + 1) * CX]
-        for ref, value, base in (
-            (low_ref, first, HALO * LANES),
-            (clow_ref, first, HALO * 16),
-            (high_ref, final, HALO * LANES),
-            (chigh_ref, final, HALO * 16),
-        ):
-            ref[base + k * NEAR : base + (k + 1) * NEAR] = value
-
-
-def prepare(info, state, diffusion, coupling, land_sea):
-    along = struct(HALO * LANES + NAT * NEAR, LANES)
-    corner = struct(HALO * 16 + NAT * NEAR, LANES)
-    return pl.pallas_call(
-        prepare_kernel,
-        in_specs=[SM] + [VM] * 4,
-        out_specs=[VM] * 7,
-        out_shape=[
-            struct(CX, LANES, LANES), struct(NAT * CX, LANES),
-            along, along, struct(16 * CX + NAT * CX, LANES), corner, corner,
-        ],
-        compiler_params=params(),
-        name="prepare",
-    )(info, state, diffusion, coupling, land_sea)
+        at = EDGE + k * NEAR
+        low_ref[at : at + NEAR] = nat_ref[k * CX : k * CX + NEAR]
+        high_ref[at : at + NEAR] = nat_ref[(k + 1) * CX - NEAR : (k + 1) * CX]
+    low_ref[EDGE_NAT:] = side_ref[0:CORNER]
+    high_ref[EDGE_NAT:] = side_ref[SIDE_ROWS - CORNER :]
+
+
+def pack(cells, nat, side):
+    return pl.pallas_call(
+        pack_kernel,
+        in_specs=[VM] * 3,
+        out_specs=[VM] * 2,
+        out_shape=[struct(EDGE_ROWS, LANES)] * 2,
+        compiler_params=params(),
+        name="pack",
+    )(cells, nat, side)
 
 
 def linear_step(planes, made, mixing, diff, gate, damp):
@@ -226,14 +250,16 @@
     return [coef_ref[k * TALL : (k + 1) * TALL] for k in range(4)]
 
 
-def gather_kernel(mix_ref, nat_ref, low_ref, high_ref, side_ref, clow_ref, chigh_ref, coef_ref, top_ref):
+def gather_kernel(mix_ref, nat_ref, low_ref, high_ref, side_ref, coef_ref, top_ref):
     def plane(k):
-        own = [high_ref[HALO * LANES + k * NEAR : HALO * LANES + (k + 1) * NEAR],
-               nat_ref[k * CX : (k + 1) * CX],
-               low_ref[HALO * LANES + k * NEAR : HALO * LANES + (k + 1) * NEAR]]
-        other = [chigh_ref[HALO * 16 + k * NEAR : HALO * 16 + (k + 1) * NEAR],
-                 side_ref[16 * CX + k * CX : 16 * CX + (k + 1) * CX],
-                 clow_ref[HALO * 16 + k * NEAR : HALO * 16 + (k + 1) * NEAR]]
+        def part(ref, base):
+            return ref[base + k * NEAR : base + (k + 1) * NEAR]
+
+        own = [part(high_ref, EDGE), nat_ref[k * CX : (k + 1) * CX], part(low_ref, EDGE)]
+        other = [
+            part(high_ref, EDGE_NAT + HALO * 16), part(side_ref, 0), part(side_ref, SIDE_NAT),
+            part(low_ref, EDGE_NAT),
+        ]
         return jnp.concatenate(
             [jnp.concatenate(own, axis=0), jnp.concatenate(other, axis=0)], axis=1
         )
@@ -252,7 +278,7 @@
 def gather(mixing, nat, halo):
     return pl.pallas_call(
         gather_kernel,
-        in_specs=[SM] + [VM] * 6,
+        in_specs=[SM] + [VM] * 4,
         out_specs=[VM] * 2,
         out_shape=[struct(4 * TALL, RING), struct(2, CX, LANES)],
         compiler_params=params(),
@@ -261,10 +287,10 @@
 
 
 def forcing(info_ref, hops, coef_ref, work):
-    a, b, l1, l2, h1, h2 = hops
-    work[0 : 4 * NEAR] = l1[...] + l2[...]
-    work[4 * NEAR : 4 * (NEAR + CX)] = a[...] + b[...]
-    work[4 * (NEAR + CX) : 4 * TALL] = h1[...] + h2[...]
+    own, low, high = hops
+    work[0 : 4 * NEAR] = low[...]
+    work[4 * NEAR : 4 * (NEAR + CX)] = own[...]
+    work[4 * (NEAR + CX) : 4 * TALL] = high[...]
     north = info_ref[1] == 1
     scale = coef_ref[3 * TALL : 4 * TALL]
     out = []
@@ -287,9 +313,9 @@
 
 def turn_kernel(*refs):
     info_ref, mix_ref, coef_ref, top_ref = refs[:4]
-    hops, routes_hbm, w_hbm = refs[4:10], refs[10:14], refs[14]
-    send_ref, resp_ref = refs[15:17]
-    routes, (w, surf, count, sems, work) = refs[17:21], refs[21:]
+    hops, routes_hbm, w_hbm = refs[4:7], refs[7:11], refs[11]
+    send_ref, resp_ref = refs[12:14]
+    routes, (w, surf, count, sems, work) = refs[14:18], refs[18:]
     fetch_start(routes_hbm, routes, w_hbm, w, sems)
     send_ref[...] = jnp.zeros_like(send_ref)
     diff, gate, damp, _ = coefs(coef_ref)
@@ -313,7 +339,7 @@
     pairs = weights.shape[0]
     return pl.pallas_call(
         turn_kernel,
-        in_specs=[SM, SM] + [VM] * 8 + [HB] * 5,
+        in_specs=[SM, SM] + [VM] * 5 + [HB] * 5,
         out_specs=[VM] * 2,
         out_shape=[struct(columns * 8, LANES), struct(6, TALL, RING)],
         scratch_shapes=pair_scratch(pairs, columns) + [pltpu.VMEM((4 * TALL, LANES), f32)],
@@ -369,8 +395,8 @@
 
 def bulk_kernel(
     mixrow_ref, mix_ref, cells_ref, coef_ref, resp_ref,
-    low_ref, high_ref, side_ref, clow_ref, chigh_ref,
-    out_ref, fa, fb, diff, gate, self_, work,
+    low_ref, high_ref, side_ref,
+    out_ref, top_ref, fa, fb, diff, gate, self_, work,
 ):
     lanes = lax.broadcasted_iota(jnp.int32, (1, LANES), 1)
     level = jnp.where(lanes >= LEV, lanes - LEV, lanes)
@@ -381,13 +407,13 @@
 
     for x in range(CX):
         fa[HALO + x, 16:144] = cells_ref[x]
-        fa[HALO + x, 8:16] = side_ref[16 * x + 8 : 16 * x + 16]
-        fa[HALO + x, 144:152] = side_ref[16 * x : 16 * x + 8]
+        fa[HALO + x, 8:16] = side_ref[SIDE + 16 * x + 8 : SIDE + 16 * x + 16]
+        fa[HALO + x, 144:152] = side_ref[SIDE + 16 * x : SIDE + 16 * x + 8]
     for j in range(HALO):
-        for at, along, corner in ((j, high_ref, chigh_ref), (HALO + CX + j, low_ref, clow_ref)):
+        for at, along, base in ((j, high_ref, EDGE_NAT), (HALO + CX + j, low_ref, EDGE_NAT + NAT * NEAR)):
             fa[at, 16:144] = along[j * LANES : (j + 1) * LANES]
-            fa[at, 8:16] = corner[16 * j + 8 : 16 * j + 16]
-            fa[at, 144:152] = corner[16 * j : 16 * j + 8]
+            fa[at, 8:16] = along[base + 16 * j + 8 : base + 16 * j + 16]
+            fa[at, 144:152] = along[base + 16 * j : base + 16 * j + 8]
 
     work[...] = jnp.zeros_like(work)
 
@@ -442,7 +468,10 @@
             planes = linear_step(planes, made, mixing, d, g, c)
         for k in range(6):
             at = (f * LEV + k) * CX
-            out_ref[at : at + CX] += planes[k][NEAR : NEAR + CX, 0:LANES]
+            full = out_ref[at : at + CX] + planes[k][NEAR : NEAR + CX, 0:LANES]
+            out_ref[at : at + CX] = full
+            if k < 3:
+                top_ref[f, k] = full
 
 
 def bulk(mixrow, mixing, cells, coef, resp, halo):
@@ -450,9 +479,9 @@
     coefficient = pltpu.VMEM((CX + 2 * HALO - 2, WIDE, LANES), f32)
     return pl.pallas_call(
         bulk_kernel,
-        in_specs=[VM, SM] + [VM] * 8,
-        out_specs=VM,
-        out_shape=struct(2 * LEV * CX, LANES),
+        in_specs=[VM, SM] + [VM] * 6,
+        out_specs=[VM, VM],
+        out_shape=[struct(2 * LEV * CX, LANES), struct(2, 3, CX, LANES)],
         scratch_shapes=[big, big] + [coefficient] * 3 + [pltpu.VMEM((LANES, LANES), f32)],
         compiler_params=params(),
         cost_estimate=pl.CostEstimate(flops=40_000_000, transcendentals=0, bytes_accessed=40_000_000),
@@ -460,29 +489,29 @@
     )(mixrow, mixing, cells, coef, resp, *halo)
 
 
-def final_kernel(info_ref, mix_ref, coef_ref, a, b, l1, l2, h1, h2, part_ref, out_ref, work):
+def final_kernel(info_ref, mix_ref, coef_ref, own, low, high, top_ref, part_ref, out_ref, work):
     diff, gate, damp, _ = coefs(coef_ref)
     mixing = [mix_ref[k] for k in range(3)]
-    force = forcing(info_ref, (a, b, l1, l2, h1, h2), coef_ref, work)
+    force = forcing(info_ref, (own, low, high), coef_ref, work)
     for f in range(2):
         planes = response(force[f], mixing, diff, gate, damp)
         for k in range(3):
-            out_ref[f, k] = part_ref[f, k] + planes[k][NEAR : NEAR + CX, 0:LANES]
-
-
-def final(info, mixing, coef, hops, part):
+            out_ref[f, k] = top_ref[f, k] + planes[k][NEAR : NEAR + CX, 0:LANES]
+
+
+def final(info, mixing, coef, hops, top, part):
     block = pl.BlockSpec((2, 3, CX, LANES), lambda i: (0, 0, 0, 0))
     return pl.pallas_call(
         final_kernel,
         grid=(1,),
-        in_specs=[SM, SM] + [VM] * 7 + [block],
+        in_specs=[SM, SM] + [VM] * 5 + [HB],
         out_specs=block,
         out_shape=struct(2, LEV, CX, LANES),
-        input_output_aliases={9: 0},
+        input_output_aliases={7: 0},
         scratch_shapes=[pltpu.VMEM((4 * TALL, LANES), f32)],
         compiler_params=params(),
         name="final",
-    )(info, mixing, coef, *hops, part)
+    )(info, mixing, coef, *hops, top, part)
 
 
 def solution(mesh):
@@ -498,24 +527,12 @@
                     pairs.append(((s * columns + g) * halves + h, (a * columns + b) * halves + c))
         return lax.ppermute(value, AXES, pairs)
 
-    def exchanged(low, high, side, clow, chigh):
+    def hopped(dense):
+        full = dense + sent(dense, lambda s, g, h: (s, g, h + 1))
         return (
-            sent(low, lambda s, g, h: (s, g - 1, h)),
-            sent(high, lambda s, g, h: (s, g + 1, h)),
-            sent(side, lambda s, g, h: (s, g, h + 1)),
-            sent(clow, lambda s, g, h: (s, g - 1, h + 1)),
-            sent(chigh, lambda s, g, h: (s, g + 1, h + 1)),
-        )
-
-    def hopped(dense):
-        first, final_ = dense[: 4 * NEAR], dense[4 * (CX - NEAR) :]
-        return (
-            sent(dense, lambda s, g, h: (1 - s, g, h)),
-            sent(dense, lambda s, g, h: (1 - s, g, h + 1)),
-            sent(final_, lambda s, g, h: (1 - s, g + 1, h)),
-            sent(final_, lambda s, g, h: (1 - s, g + 1, h + 1)),
-            sent(first, lambda s, g, h: (1 - s, g - 1, h)),
-            sent(first, lambda s, g, h: (1 - s, g - 1, h + 1)),
+            sent(full, lambda s, g, h: (1 - s, g, h)),
+            sent(full[4 * (CX - NEAR) :], lambda s, g, h: (1 - s, g + 1, h)),
+            sent(full[: 4 * NEAR], lambda s, g, h: (1 - s, g - 1, h)),
         )
 
     def body(
@@ -528,22 +545,29 @@
         routes = (route_tile[0, 0, :, 0], route_src[0, 0], route_dst[0, 0], pair_cols[0, 0])
         weights = intersection[0, 0]
 
+        cells, nat, side = prepare(
+            info, state.reshape(-1, LANES), diffusion[0], coupling[0], land_sea[0]
+        )
+        side = sent(side, lambda s, g, h: (s, g, h + 1))
         send = first_contributions(routes, weights, state[0], columns)
+        send, side = lax.optimization_barrier((send, side))
         got = lax.all_to_all(send, "gx", 0, 0, tiled=True)
-        cells, nat, *edges = prepare(
-            info, state.reshape(-1, LANES), diffusion[0], coupling[0], land_sea[0]
-        )
-        halo = exchanged(*edges)
+        low, high = pack(cells, nat, side)
+        halo = (
+            sent(low, lambda s, g, h: (s, g - 1, h)),
+            sent(high, lambda s, g, h: (s, g + 1, h)),
+            side,
+        )
         coef, top = gather(mixing, nat, halo)
         dense, marks = densify(got.reshape(-1, LANES), None)
         hops = hopped(dense)
         send, resp = turn(info, mixing, coef, top, hops, routes, weights, columns)
 
         got = lax.all_to_all(send, "gx", 0, 0, tiled=True)
-        part = bulk(mixrow, mixing, cells, coef, resp, halo)
-        got, part = lax.optimization_barrier((got, part))
+        part, low = bulk(mixrow, mixing, cells, coef, resp, halo)
+        got, part, low = lax.optimization_barrier((got, part, low))
         hops = hopped(densify(got, marks))
-        out = final(info, mixing, coef, hops, part.reshape(state.shape[1:]))
+        out = final(info, mixing, coef, hops, low, part.reshape(state.shape[1:]))
         return out[None]
 
     spec = P("comp", "gx", "gy")

time: 96.6 us -> 91.1 us (0.943)
  starting transfers between devices: 50.5 us -> 34.1 us
  waiting for transfers between devices: 23 us -> 33.9 us
    ppermute x17 -> x11, starting transfers between devices: 33 us -> 16.9 us  [sent(): return lax.ppermute(value, AXES, pairs)]
    all_to_all x2, waiting for transfers between devices: 4.21 us -> 11.1 us  [body(): got = lax.all_to_all(send, 'gx', 0, 0, tiled=True)]
    ppermute x17 -> x11, waiting for transfers between devices: 18.8 us -> 22.8 us  [sent(): return lax.ppermute(value, AXES, pairs)]
    pallas_call x5 -> x6, Pallas kernels: 17.6 us -> 18.4 us  [the longest x1 9.06 us: bulk(): pl.pallas_call(bulk_kernel, in_specs=[VM, SM] + [VM] * 6, out_specs=[VM,...]
  transfers between devices with their start and end apart: 19 -> 13, of which waited for: 8 -> 9; matrix products, arithmetic and copies ran while one was open for 0% -> 0% of each run, Pallas kernels for 12% -> 16%
where the time goes in v1:
time: 91.1 us; the launch traced here: 90.9 us
  starting transfers between devices  34.1 us (37%)
  waiting for transfers between devices  33.9 us (37%)
  Pallas kernels  22.6 us (25%)
    ppermute x11, waiting for transfers between devices, sent(): return lax.ppermute(value, AXES, pairs)  22.8 us
    all_to_all x2, starting transfers between devices, body(): got = lax.all_to_all(send, 'gx', 0, 0, tiled=True)  17.2 us
    ppermute x11, starting transfers between devices, sent(): return lax.ppermute(value, AXES, pairs)  16.9 us
    all_to_all x2, waiting for transfers between devices, body(): got = lax.all_to_all(send, 'gx', 0, 0, tiled=True)  11.1 us
    pallas_call x1, Pallas kernels, bulk(): pl.pallas_call(bulk_kernel, in_specs=[VM, SM] + [VM] * 6, out_specs=[VM,...  9.06 us
    pallas_call x1, Pallas kernels, turn(): pl.pallas_call(turn_kernel, in_specs=[SM, SM] + [VM] * 5 + [HB] * 5, out_...  3.92 us
    pallas_call x1, Pallas kernels, first_contributions(): pl.pallas_call(first_kernel, in_specs=[HB] * 6, out_specs=VM, out_shape=s...  3.65 us
    pallas_call x1, Pallas kernels, prepare(): pl.pallas_call(prepare_kernel, in_specs=[SM] + [HB] * 4, out_specs=[VM] *...  2.23 us
  transfers between devices with their start and end apart: 13, of which 9 were waited for; matrix products, arithmetic and copies ran while one was open for 0% of the time, Pallas kernels for 16%

profile of v1, /device:TPU:6, one launch (start us, length us, event | category | flops | bytes accessed | tf_op | source)
XLA Modules:
  0.0 90.9 jit_solution(18066503593322743290)
XLA Ops:
  0.0 0.1 pad_add_fusion.info_ref.refs_0_
  0.1 2.2 %prepare.1 = (f32[16,128,128]{2,1,0:T(8,128)S(1)}, f32[192,128]{1,0:T(8,128)S(1)}, f32[448,128]{1,0:T(8,128)S(1)}) custom-call(s32[2]{0:T(128)S(1)} %pad_add_fusion.info_ref.refs_0_, f32[2048,128]{1,0:T(8,128)} %bitcast.26, f32[16,128]{1,0:T(8,128)} %bitcast.29, f32[16,128]{1,0:T(8,128)} %bitcast.30, s32[16,128]{1,0:T(8,128)} %bitcast.31), custom_call_target="tpu_custom_call" | custom-call | tf_op jit(solution)/shard_map/prepare/pallas_call | solution.py:183
  2.3 0.9 %collective-permute-start = (f32[448,128]{1,0:T(8,128)S(1)}, f32[448,128]{1,0:T(8,128)S(1)}, u32[]{:S(2)}, u32[]{:S(2)}) collective-permute-start(f32[448,128]{1,0:T(8,128)S(1)} %get-tuple-element.25), channel_id=1, source_target_pairs={{0,1},{1,0},{2,3},{3,2},{4,5},{5,4},{6,7},{7,6},{8,9},{9,8},{10,11... | collective-permute-start | bytes 688136 | tf_op jit(solution)/shard_map/ppermute | solution.py:528
  3.2 0.0 copy-start
  3.2 3.7 %contrib.1 = f32[576,1,128]{2,1,0:T(1,128)} custom-call(s32[64]{0:T(128)} %bitcast.32, s32[64]{0:T(128)} %bitcast.34, s32[64]{0:T(128)} %bitcast.36, s32[64]{0:T(128)} %bitcast.38, bf16[64,128,128]{2,1,0:T(8,128)(2,1)} %bitcast.24, f32[2,64,16,128]{3,2,1,0:T(8,128)} %bitcast.27), custom_call_target="tpu_custom_call" | custom-call | tf_op jit(solution)/shard_map/contrib/pallas_call | solution.py:124
  6.9 2.9 %collective-permute-done.side_ref = f32[448,128]{1,0:T(8,128)S(1)} collective-permute-done((f32[448,128]{1,0:T(8,128)S(1)}, f32[448,128]{1,0:T(8,128)S(1)}, u32[]{:S(2)}, u32[]{:S(2)}) %collective-permute-start) | collective-permute-done | bytes 229408 | tf_op jit(solution)/shard_map/ppermute | solution.py:528
  9.7 12.1 %all-to-all-start = ((f32[576,1,128]{2,1,0:T(1,128)}), f32[576,1,128]{2,1,0:T(1,128)S(1)}, u32[]{:S(2)}, u32[]{:S(2)}) async-start(f32[576,1,128]{2,1,0:T(1,128)} %contrib.1), calls=%async_computation | async-start | bytes 589824 | tf_op jit(solution)/shard_map/all_to_all | solution.py:554
  21.9 1.1 %pack.1 = (f32[1056,128]{1,0:T(8,128)}, f32[1056,128]{1,0:T(8,128)}) custom-call(f32[16,128,128]{2,1,0:T(8,128)S(1)} %get-tuple-element.24.cells_ref, f32[192,128]{1,0:T(8,128)S(1)} %get-tuple-element.23.nat_ref, f32[448,128]{1,0:T(8,128)S(1)} %collective-permute-done.side_ref), custom_call_target="tpu_custom_call" | custom-call | tf_op jit(solution)/shard_map/pack/pallas_call | solution.py:212
  22.9 4.9 %collective-permute-start.1 = (f32[1056,128]{1,0:T(8,128)}, f32[1056,128]{1,0:T(8,128)S(1)}, u32[]{:S(2)}, u32[]{:S(2)}) collective-permute-start(f32[1056,128]{1,0:T(8,128)} %get-tuple-element.27), channel_id=1, source_target_pairs={{0,126},{1,127},{2,0},{3,1},{4,2},{5,3},{6,4},{7,5},{8,6},{9,7},{1... | collective-permute-start | bytes 1622024 | tf_op jit(solution)/shard_map/ppermute | solution.py:528
  27.9 0.0 collective-permute-start.2
  27.9 7.4 %all-to-all-done = f32[576,1,128]{2,1,0:T(1,128)S(1)} async-done(((f32[576,1,128]{2,1,0:T(1,128)}), f32[576,1,128]{2,1,0:T(1,128)S(1)}, u32[]{:S(2)}, u32[]{:S(2)}) %all-to-all-start) | async-done | bytes 294944 | tf_op jit(solution)/shard_map/all_to_all | solution.py:554
  35.3 0.3 densify.2
  35.6 0.9 collective-permute-start.3
  36.4 3.1 %collective-permute-done.3 = f32[64,128]{1,0:T(8,128)S(1)} collective-permute-done((f32[64,128]{1,0:T(8,128)S(1)}, f32[64,128]{1,0:T(8,128)S(1)}, u32[]{:S(2)}, u32[]{:S(2)}) %collective-permute-start.3) | collective-permute-done | bytes 32800 | tf_op jit(solution)/shard_map/ppermute | solution.py:528
  39.5 1.4 %collective-permute-start.4 = (f32[64,128]{1,0:T(8,128)S(1)}, f32[64,128]{1,0:T(8,128)S(1)}, u32[]{:S(2)}, u32[]{:S(2)}) collective-permute-start(f32[64,128]{1,0:T(8,128)S(1)} %add.6), channel_id=1, source_target_pairs={{0,128},{1,129},{2,130},{3,131},{4,132},{5,133},{6,134},{7,135},{8... | collective-permute-start | bytes 98312 | tf_op jit(solution)/shard_map/ppermute | solution.py:528
  40.9 1.8 %collective-permute-start.6 = (f32[32,128]{1,0:T(8,128)S(1)}, f32[32,128]{1,0:T(8,128)S(1)}, u32[]{:S(2)}, u32[]{:S(2)}) collective-permute-start(f32[32,128]{1,0:T(8,128)S(1)} %get-tuple-element.43), channel_id=1, source_target_pairs={{0,254},{1,255},{2,128},{3,129},{4,130},{5,131},{6,132},{7,133},{8... | collective-permute-start | bytes 49160 | tf_op jit(solution)/shard_map/ppermute | solution.py:528
  42.8 1.4 %collective-permute-start.5 = (f32[32,128]{1,0:T(8,128)S(1)}, f32[32,128]{1,0:T(8,128)S(1)}, u32[]{:S(2)}, u32[]{:S(2)}) collective-permute-start(f32[32,128]{1,0:T(8,128)S(1)} %get-tuple-element.44), channel_id=1, source_target_pairs={{0,130},{1,131},{2,132},{3,133},{4,134},{5,135},{6,136},{7,137},{8... | collective-permute-start | bytes 49160 | tf_op jit(solution)/shard_map/ppermute | solution.py:528
  44.2 0.0 collective-permute-done.1.low_ref
  44.2 0.0 collective-permute-done.2.high_ref
  44.2 0.0 copy-done
  44.2 0.8 gather.1
  45.0 0.6 collective-permute-done.6.refs_6_
  45.6 6.0 %collective-permute-done.5.refs_5_ = f32[32,128]{1,0:T(8,128)S(1)} collective-permute-done((f32[32,128]{1,0:T(8,128)S(1)}, f32[32,128]{1,0:T(8,128)S(1)}, u32[]{:S(2)}, u32[]{:S(2)}) %collective-permute-start.5) | collective-permute-done | bytes 16416 | tf_op jit(solution)/shard_map/ppermute | solution.py:528
  51.7 0.0 collective-permute-done.4.refs_4_
  51.7 3.9 %turn.1 = (f32[512,128]{1,0:T(8,128)}, f32[6,32,256]{2,1,0:T(8,128)S(1)}) custom-call(s32[2]{0:T(128)S(1)} %pad_add_fusion.info_ref.refs_0_, f32[64]{0:T(128)S(1)} %bitcast.21, f32[128,256]{1,0:T(8,128)S(1)} %get-tuple-element.29.refs_2_.coef_ref, f32[2,16,128]{2,1,0:T(8,128)S(1)} %get-tuple-element.30.refs_3_, ...), custom_call_target="tpu_custom_call" | custom-call | tf_op jit(solution)/shard_map/turn/pallas_call | solution.py:340
  55.6 5.1 %all-to-all-start.1 = ((f32[64,8,128]{2,1,0:T(8,128)}), f32[64,8,128]{2,1,0:T(8,128)S(1)}, u32[]{:S(2)}, u32[]{:S(2)}) async-start(f32[64,8,128]{2,1,0:T(8,128)} %bitcast.14), calls=%async_computation.1 | async-start | bytes 524288 | tf_op jit(solution)/shard_map/all_to_all | solution.py:566
  60.7 0.1 pad_maximum_fusion.mixrow_ref
  60.8 9.1 %bulk.1 = (f32[2048,128]{1,0:T(8,128)}, f32[2,3,16,128]{3,2,1,0:T(8,128)S(1)}) custom-call(f32[1,128]{1,0:T(1,128)S(1)} %pad_maximum_fusion.mixrow_ref, f32[64]{0:T(128)S(1)} %bitcast.22, f32[16,128,128]{2,1,0:T(8,128)S(1)} %get-tuple-element.24.cells_ref, f32[128,256]{1,0:T(8,128)S(1)} %get-tuple-element.29.refs_2_.coef_ref, ...), custom_call_target="tpu_custom_call" | custom-call | flops 40000000 | bytes 40000000 | tf_op jit(solution)/shard_map/bulk/pallas_call | solution.py:480
  69.9 3.6 %all-to-all-done.1 = f32[64,8,128]{2,1,0:T(8,128)S(1)} async-done(((f32[64,8,128]{2,1,0:T(8,128)}), f32[64,8,128]{2,1,0:T(8,128)S(1)}, u32[]{:S(2)}, u32[]{:S(2)}) %all-to-all-start.1) | async-done | bytes 262176 | tf_op jit(solution)/shard_map/all_to_all | solution.py:566
  73.5 0.2 densify.3
  73.7 0.8 collective-permute-start.7
  74.6 3.1 %collective-permute-done.7 = f32[64,128]{1,0:T(8,128)S(1)} collective-permute-done((f32[64,128]{1,0:T(8,128)S(1)}, f32[64,128]{1,0:T(8,128)S(1)}, u32[]{:S(2)}, u32[]{:S(2)}) %collective-permute-start.7) | collective-permute-done | bytes 32800 | tf_op jit(solution)/shard_map/ppermute | solution.py:528
  77.7 1.4 %collective-permute-start.8 = (f32[64,128]{1,0:T(8,128)S(1)}, f32[64,128]{1,0:T(8,128)S(1)}, u32[]{:S(2)}, u32[]{:S(2)}) collective-permute-start(f32[64,128]{1,0:T(8,128)S(1)} %add.7), channel_id=1, source_target_pairs={{0,128},{1,129},{2,130},{3,131},{4,132},{5,133},{6,134},{7,135},{8... | collective-permute-start | bytes 98312 | tf_op jit(solution)/shard_map/ppermute | solution.py:528
  79.1 1.5 %collective-permute-start.10 = (f32[32,128]{1,0:T(8,128)S(1)}, f32[32,128]{1,0:T(8,128)S(1)}, u32[]{:S(2)}, u32[]{:S(2)}) collective-permute-start(f32[32,128]{1,0:T(8,128)S(1)} %get-tuple-element.41), channel_id=1, source_target_pairs={{0,254},{1,255},{2,128},{3,129},{4,130},{5,131},{6,132},{7,133},{8... | collective-permute-start | bytes 49160 | tf_op jit(solution)/shard_map/ppermute | solution.py:528
  80.6 1.7 %collective-permute-start.9 = (f32[32,128]{1,0:T(8,128)S(1)}, f32[32,128]{1,0:T(8,128)S(1)}, u32[]{:S(2)}, u32[]{:S(2)}) collective-permute-start(f32[32,128]{1,0:T(8,128)S(1)} %get-tuple-element.42), channel_id=1, source_target_pairs={{0,130},{1,131},{2,132},{3,133},{4,134},{5,135},{6,136},{7,137},{8... | collective-permute-start | bytes 49160 | tf_op jit(solution)/shard_map/ppermute | solution.py:528
  82.3 1.5 %collective-permute-done.10.high = f32[32,128]{1,0:T(8,128)S(1)} collective-permute-done((f32[32,128]{1,0:T(8,128)S(1)}, f32[32,128]{1,0:T(8,128)S(1)}, u32[]{:S(2)}, u32[]{:S(2)}) %collective-permute-start.10) | collective-permute-done | bytes 16416 | tf_op jit(solution)/shard_map/ppermute | solution.py:528
  83.8 5.7 %collective-permute-done.9.low = f32[32,128]{1,0:T(8,128)S(1)} collective-permute-done((f32[32,128]{1,0:T(8,128)S(1)}, f32[32,128]{1,0:T(8,128)S(1)}, u32[]{:S(2)}, u32[]{:S(2)}) %collective-permute-start.9) | collective-permute-done | bytes 16416 | tf_op jit(solution)/shard_map/ppermute | solution.py:528
  89.5 0.0 collective-permute-done.8.own
  89.5 1.4 %final.1 = f32[2,64,16,128]{3,2,1,0:T(8,128)} custom-call(s32[2]{0:T(128)S(1)} %pad_add_fusion.info_ref.refs_0_, f32[64]{0:T(128)S(1)} %bitcast.23, f32[128,256]{1,0:T(8,128)S(1)} %get-tuple-element.29.refs_2_.coef_ref, f32[64,128]{1,0:T(8,128)S(1)} %collective-permute-done.8.own, ...), custom_call_target="tpu_custom_call", output_to_operand_aliasing={{}: (7, {})} | custom-call | tf_op jit(solution)/shard_map/final/pallas_call | solution.py:504
  (4 shorter events, 0.0 us)
Async XLA Ops:
  2.3 7.4 %collective-permute-start = (f32[448,128]{1,0:T(8,128)S(1)}, f32[448,128]{1,0:T(8,128)S(1)}, u32[]{:S(2)}, u32[]{:S(2)}) collective-permute-start(f32[448,128]{1,0:T(8,128)S(1)} %get-tuple-element.25), channel_id=1, source_target_pairs={{0,1},{1,0},{2,3},{3,2},{4,5},{5,4},{6,7},{7,6},{8,9},{9,8},{10,11... | collective-permute-start | bytes 688136 | tf_op jit(solution)/shard_map/ppermute | solution.py:528
  3.2 41.0 %copy-start = (f32[1,64]{1,0:T(1,128)S(1)}, f32[1,64]{1,0:T(1,128)}, u32[]{:S(2)}) copy-start(f32[1,64]{1,0:T(1,128)} %param.12) | copy-start | bytes 772
  9.7 25.6 %all-to-all-start = ((f32[576,1,128]{2,1,0:T(1,128)}), f32[576,1,128]{2,1,0:T(1,128)S(1)}, u32[]{:S(2)}, u32[]{:S(2)}) async-start(f32[576,1,128]{2,1,0:T(1,128)} %contrib.1), calls=%async_computation | async-start | bytes 589824 | tf_op jit(solution)/shard_map/all_to_all | solution.py:554
  22.9 21.3 %collective-permute-start.1 = (f32[1056,128]{1,0:T(8,128)}, f32[1056,128]{1,0:T(8,128)S(1)}, u32[]{:S(2)}, u32[]{:S(2)}) collective-permute-start(f32[1056,128]{1,0:T(8,128)} %get-tuple-element.27), channel_id=1, source_target_pairs={{0,126},{1,127},{2,0},{3,1},{4,2},{5,3},{6,4},{7,5},{8,6},{9,7},{1... | collective-permute-start | bytes 1622024 | tf_op jit(solution)/shard_map/ppermute | solution.py:528
  27.9 16.3 %collective-permute-start.2 = (f32[1056,128]{1,0:T(8,128)}, f32[1056,128]{1,0:T(8,128)S(1)}, u32[]{:S(2)}, u32[]{:S(2)}) collective-permute-start(f32[1056,128]{1,0:T(8,128)} %get-tuple-element.28), channel_id=1, source_target_pairs={{0,2},{1,3},{2,4},{3,5},{4,6},{5,7},{6,8},{7,9},{8,10},{9,11},{10,... | collective-permute-start | bytes 1622024 | tf_op jit(solution)/shard_map/ppermute | solution.py:528
  35.6 3.9 %collective-permute-start.3 = (f32[64,128]{1,0:T(8,128)S(1)}, f32[64,128]{1,0:T(8,128)S(1)}, u32[]{:S(2)}, u32[]{:S(2)}) collective-permute-start(f32[64,128]{1,0:T(8,128)S(1)} %get-tuple-element.32), channel_id=1, source_target_pairs={{0,1},{1,0},{2,3},{3,2},{4,5},{5,4},{6,7},{7,6},{8,9},{9,8},{10,11... | collective-permute-start | bytes 98312 | tf_op jit(solution)/shard_map/ppermute | solution.py:528
  39.5 12.1 %collective-permute-start.4 = (f32[64,128]{1,0:T(8,128)S(1)}, f32[64,128]{1,0:T(8,128)S(1)}, u32[]{:S(2)}, u32[]{:S(2)}) collective-permute-start(f32[64,128]{1,0:T(8,128)S(1)} %add.6), channel_id=1, source_target_pairs={{0,128},{1,129},{2,130},{3,131},{4,132},{5,133},{6,134},{7,135},{8... | collective-permute-start | bytes 98312 | tf_op jit(solution)/shard_map/ppermute | solution.py:528
  40.9 4.7 %collective-permute-start.6 = (f32[32,128]{1,0:T(8,128)S(1)}, f32[32,128]{1,0:T(8,128)S(1)}, u32[]{:S(2)}, u32[]{:S(2)}) collective-permute-start(f32[32,128]{1,0:T(8,128)S(1)} %get-tuple-element.43), channel_id=1, source_target_pairs={{0,254},{1,255},{2,128},{3,129},{4,130},{5,131},{6,132},{7,133},{8... | collective-permute-start | bytes 49160 | tf_op jit(solution)/shard_map/ppermute | solution.py:528
  42.8 8.9 %collective-permute-start.5 = (f32[32,128]{1,0:T(8,128)S(1)}, f32[32,128]{1,0:T(8,128)S(1)}, u32[]{:S(2)}, u32[]{:S(2)}) collective-permute-start(f32[32,128]{1,0:T(8,128)S(1)} %get-tuple-element.44), channel_id=1, source_target_pairs={{0,130},{1,131},{2,132},{3,133},{4,134},{5,135},{6,136},{7,137},{8... | collective-permute-start | bytes 49160 | tf_op jit(solution)/shard_map/ppermute | solution.py:528
  55.6 17.9 %all-to-all-start.1 = ((f32[64,8,128]{2,1,0:T(8,128)}), f32[64,8,128]{2,1,0:T(8,128)S(1)}, u32[]{:S(2)}, u32[]{:S(2)}) async-start(f32[64,8,128]{2,1,0:T(8,128)} %bitcast.14), calls=%async_computation.1 | async-start | bytes 524288 | tf_op jit(solution)/shard_map/all_to_all | solution.py:566
  73.7 3.9 %collective-permute-start.7 = (f32[64,128]{1,0:T(8,128)S(1)}, f32[64,128]{1,0:T(8,128)S(1)}, u32[]{:S(2)}, u32[]{:S(2)}) collective-permute-start(f32[64,128]{1,0:T(8,128)S(1)} %densify.3), channel_id=1, source_target_pairs={{0,1},{1,0},{2,3},{3,2},{4,5},{5,4},{6,7},{7,6},{8,9},{9,8},{10,11... | collective-permute-start | bytes 98312 | tf_op jit(solution)/shard_map/ppermute | solution.py:528
  77.7 11.8 %collective-permute-start.8 = (f32[64,128]{1,0:T(8,128)S(1)}, f32[64,128]{1,0:T(8,128)S(1)}, u32[]{:S(2)}, u32[]{:S(2)}) collective-permute-start(f32[64,128]{1,0:T(8,128)S(1)} %add.7), channel_id=1, source_target_pairs={{0,128},{1,129},{2,130},{3,131},{4,132},{5,133},{6,134},{7,135},{8... | collective-permute-start | bytes 98312 | tf_op jit(solution)/shard_map/ppermute | solution.py:528
  79.1 4.7 %collective-permute-start.10 = (f32[32,128]{1,0:T(8,128)S(1)}, f32[32,128]{1,0:T(8,128)S(1)}, u32[]{:S(2)}, u32[]{:S(2)}) collective-permute-start(f32[32,128]{1,0:T(8,128)S(1)} %get-tuple-element.41), channel_id=1, source_target_pairs={{0,254},{1,255},{2,128},{3,129},{4,130},{5,131},{6,132},{7,133},{8... | collective-permute-start | bytes 49160 | tf_op jit(solution)/shard_map/ppermute | solution.py:528
  80.6 8.9 %collective-permute-start.9 = (f32[32,128]{1,0:T(8,128)S(1)}, f32[32,128]{1,0:T(8,128)S(1)}, u32[]{:S(2)}, u32[]{:S(2)}) collective-permute-start(f32[32,128]{1,0:T(8,128)S(1)} %get-tuple-element.42), channel_id=1, source_target_pairs={{0,130},{1,131},{2,132},{3,133},{4,134},{5,135},{6,136},{7,137},{8... | collective-permute-start | bytes 49160 | tf_op jit(solution)/shard_map/ppermute | solution.py:528

commit v2 on v1

--- a/solution.py
+++ b/solution.py
@@ -135,11 +135,11 @@
 
 EDGE = HALO * LANES
 EDGE_NAT = EDGE + NAT * NEAR
-EDGE_ROWS = EDGE_NAT + NAT * NEAR + HALO * 16
+EDGE_ROWS = EDGE_NAT + NAT * NEAR + HALO * 2 * HALO
 SIDE = NAT * NEAR
-SIDE_NAT = SIDE + 16 * CX
+SIDE_NAT = SIDE + 2 * HALO * CX
 SIDE_ROWS = SIDE_NAT + NAT * NEAR
-CORNER = NAT * NEAR + HALO * 16
+CORNER = NAT * NEAR + HALO * 2 * HALO
 
 
 def prepare_kernel(
@@ -173,9 +173,9 @@
     for x in range(CX):
         row = state_ref[pl.ds(x, LANES, stride=CX), :].T
         cells_ref[x] = row
-        at = SIDE + 16 * x
-        side_ref[at : at + 8] = row[0:8]
-        side_ref[at + 8 : at + 16] = row[120:128]
+        at = SIDE + 2 * HALO * x
+        side_ref[at : at + HALO] = row[0:HALO]
+        side_ref[at + HALO : at + 2 * HALO] = row[LANES - HALO :]
 
 
 def prepare(info, state, diffusion, coupling, land_sea):
@@ -257,7 +257,7 @@
 
         own = [part(high_ref, EDGE), nat_ref[k * CX : (k + 1) * CX], part(low_ref, EDGE)]
         other = [
-            part(high_ref, EDGE_NAT + HALO * 16), part(side_ref, 0), part(side_ref, SIDE_NAT),
+            part(high_ref, EDGE_NAT + HALO * 2 * HALO), part(side_ref, 0), part(side_ref, SIDE_NAT),
             part(low_ref, EDGE_NAT),
         ]
         return jnp.concatenate(
@@ -406,14 +406,16 @@
     mix_mid = -(mix_up + mix_low)
 
     for x in range(CX):
+        at = SIDE + 2 * HALO * x
         fa[HALO + x, 16:144] = cells_ref[x]
-        fa[HALO + x, 8:16] = side_ref[SIDE + 16 * x + 8 : SIDE + 16 * x + 16]
-        fa[HALO + x, 144:152] = side_ref[SIDE + 16 * x : SIDE + 16 * x + 8]
+        fa[HALO + x, 16 - HALO : 16] = side_ref[at + HALO : at + 2 * HALO]
+        fa[HALO + x, 144 : 144 + HALO] = side_ref[at : at + HALO]
     for j in range(HALO):
-        for at, along, base in ((j, high_ref, EDGE_NAT), (HALO + CX + j, low_ref, EDGE_NAT + NAT * NEAR)):
-            fa[at, 16:144] = along[j * LANES : (j + 1) * LANES]
-            fa[at, 8:16] = along[base + 16 * j + 8 : base + 16 * j + 16]
-            fa[at, 144:152] = along[base + 16 * j : base + 16 * j + 8]
+        for x, along, base in ((j, high_ref, EDGE_NAT), (HALO + CX + j, low_ref, EDGE_NAT + NAT * NEAR)):
+            at = base + 2 * HALO * j
+            fa[x, 16:144] = along[j * LANES : (j + 1) * LANES]
+            fa[x, 16 - HALO : 16] = along[at + HALO : at + 2 * HALO]
+            fa[x, 144 : 144 + HALO] = along[at : at + HALO]
 
     work[...] = jnp.zeros_like(work)
 

time: 91.1 us -> 90.4 us (level)
  no operation moved by 1% of the time
where the time goes in v2:
time: 90.4 us; the launch traced here: 90.2 us
  starting transfers between devices  34.1 us (38%)
  waiting for transfers between devices  33.4 us (37%)
  Pallas kernels  22.4 us (25%)
    ppermute x11, waiting for transfers between devices, sent(): return lax.ppermute(value, AXES, pairs)  22.1 us
    all_to_all x2, starting transfers between devices, body(): got = lax.all_to_all(send, 'gx', 0, 0, tiled=True)  17.2 us
    ppermute x11, starting transfers between devices, sent(): return lax.ppermute(value, AXES, pairs)  16.9 us
    all_to_all x2, waiting for transfers between devices, body(): got = lax.all_to_all(send, 'gx', 0, 0, tiled=True)  11.3 us
    pallas_call x1, Pallas kernels, bulk(): pl.pallas_call(bulk_kernel, in_specs=[VM, SM] + [VM] * 6, out_specs=[VM,...  9.07 us
    pallas_call x1, Pallas kernels, turn(): pl.pallas_call(turn_kernel, in_specs=[SM, SM] + [VM] * 5 + [HB] * 5, out_...  3.92 us
    pallas_call x1, Pallas kernels, first_contributions(): pl.pallas_call(first_kernel, in_specs=[HB] * 6, out_specs=VM, out_shape=s...  3.66 us
    pallas_call x1, Pallas kernels, prepare(): pl.pallas_call(prepare_kernel, in_specs=[SM] + [HB] * 4, out_specs=[VM] *...  2.23 us
  transfers between devices with their start and end apart: 13, of which 9 were waited for; matrix products, arithmetic and copies ran while one was open for 0% of the time, Pallas kernels for 16%

profile of v2, /device:TPU:6, one launch (start us, length us, event | category | flops | bytes accessed | tf_op | source)
XLA Modules:
  0.0 90.2 jit_solution(6146924702790826282)
XLA Ops:
  0.0 0.1 pad_add_fusion.info_ref.refs_0_
  0.1 2.2 %prepare.1 = (f32[16,128,128]{2,1,0:T(8,128)S(1)}, f32[192,128]{1,0:T(8,128)S(1)}, f32[384,128]{1,0:T(8,128)S(1)}) custom-call(s32[2]{0:T(128)S(1)} %pad_add_fusion.info_ref.refs_0_, f32[2048,128]{1,0:T(8,128)} %bitcast.26, f32[16,128]{1,0:T(8,128)} %bitcast.29, f32[16,128]{1,0:T(8,128)} %bitcast.30, s32[16,128]{1,0:T(8,128)} %bitcast.31), custom_call_target="tpu_custom_call" | custom-call | tf_op jit(solution)/shard_map/prepare/pallas_call | solution.py:183
  2.3 0.9 %collective-permute-start = (f32[384,128]{1,0:T(8,128)S(1)}, f32[384,128]{1,0:T(8,128)S(1)}, u32[]{:S(2)}, u32[]{:S(2)}) collective-permute-start(f32[384,128]{1,0:T(8,128)S(1)} %get-tuple-element.25), channel_id=1, source_target_pairs={{0,1},{1,0},{2,3},{3,2},{4,5},{5,4},{6,7},{7,6},{8,9},{9,8},{10,11... | collective-permute-start | bytes 589832 | tf_op jit(solution)/shard_map/ppermute | solution.py:530
  3.2 0.0 copy-start
  3.2 3.7 %contrib.1 = f32[576,1,128]{2,1,0:T(1,128)} custom-call(s32[64]{0:T(128)} %bitcast.32, s32[64]{0:T(128)} %bitcast.34, s32[64]{0:T(128)} %bitcast.36, s32[64]{0:T(128)} %bitcast.38, bf16[64,128,128]{2,1,0:T(8,128)(2,1)} %bitcast.24, f32[2,64,16,128]{3,2,1,0:T(8,128)} %bitcast.27), custom_call_target="tpu_custom_call" | custom-call | tf_op jit(solution)/shard_map/contrib/pallas_call | solution.py:124
  6.9 2.1 %collective-permute-done.side_ref = f32[384,128]{1,0:T(8,128)S(1)} collective-permute-done((f32[384,128]{1,0:T(8,128)S(1)}, f32[384,128]{1,0:T(8,128)S(1)}, u32[]{:S(2)}, u32[]{:S(2)}) %collective-permute-start) | collective-permute-done | bytes 196640 | tf_op jit(solution)/shard_map/ppermute | solution.py:530
  9.0 12.1 %all-to-all-start = ((f32[576,1,128]{2,1,0:T(1,128)}), f32[576,1,128]{2,1,0:T(1,128)S(1)}, u32[]{:S(2)}, u32[]{:S(2)}) async-start(f32[576,1,128]{2,1,0:T(1,128)} %contrib.1), calls=%async_computation | async-start | bytes 589824 | tf_op jit(solution)/shard_map/all_to_all | solution.py:556
  21.2 0.9 pack.1
  22.0 4.9 %collective-permute-start.1 = (f32[1032,128]{1,0:T(8,128)}, f32[1032,128]{1,0:T(8,128)S(1)}, u32[]{:S(2)}, u32[]{:S(2)}) collective-permute-start(f32[1032,128]{1,0:T(8,128)} %get-tuple-element.27), channel_id=1, source_target_pairs={{0,126},{1,127},{2,0},{3,1},{4,2},{5,3},{6,4},{7,5},{8,6},{9,7},{1... | collective-permute-start | bytes 1585160 | tf_op jit(solution)/shard_map/ppermute | solution.py:530
  27.0 0.0 collective-permute-start.2
  27.0 7.6 %all-to-all-done = f32[576,1,128]{2,1,0:T(1,128)S(1)} async-done(((f32[576,1,128]{2,1,0:T(1,128)}), f32[576,1,128]{2,1,0:T(1,128)S(1)}, u32[]{:S(2)}, u32[]{:S(2)}) %all-to-all-start) | async-done | bytes 294944 | tf_op jit(solution)/shard_map/all_to_all | solution.py:556
  34.6 0.3 densify.2
  34.9 0.9 collective-permute-start.3
  35.7 3.1 %collective-permute-done.3 = f32[64,128]{1,0:T(8,128)S(1)} collective-permute-done((f32[64,128]{1,0:T(8,128)S(1)}, f32[64,128]{1,0:T(8,128)S(1)}, u32[]{:S(2)}, u32[]{:S(2)}) %collective-permute-start.3) | collective-permute-done | bytes 32800 | tf_op jit(solution)/shard_map/ppermute | solution.py:530
  38.8 1.4 %collective-permute-start.4 = (f32[64,128]{1,0:T(8,128)S(1)}, f32[64,128]{1,0:T(8,128)S(1)}, u32[]{:S(2)}, u32[]{:S(2)}) collective-permute-start(f32[64,128]{1,0:T(8,128)S(1)} %add.6), channel_id=1, source_target_pairs={{0,128},{1,129},{2,130},{3,131},{4,132},{5,133},{6,134},{7,135},{8... | collective-permute-start | bytes 98312 | tf_op jit(solution)/shard_map/ppermute | solution.py:530
  40.2 1.8 %collective-permute-start.6 = (f32[32,128]{1,0:T(8,128)S(1)}, f32[32,128]{1,0:T(8,128)S(1)}, u32[]{:S(2)}, u32[]{:S(2)}) collective-permute-start(f32[32,128]{1,0:T(8,128)S(1)} %get-tuple-element.43), channel_id=1, source_target_pairs={{0,254},{1,255},{2,128},{3,129},{4,130},{5,131},{6,132},{7,133},{8... | collective-permute-start | bytes 49160 | tf_op jit(solution)/shard_map/ppermute | solution.py:530
  42.1 1.4 %collective-permute-start.5 = (f32[32,128]{1,0:T(8,128)S(1)}, f32[32,128]{1,0:T(8,128)S(1)}, u32[]{:S(2)}, u32[]{:S(2)}) collective-permute-start(f32[32,128]{1,0:T(8,128)S(1)} %get-tuple-element.44), channel_id=1, source_target_pairs={{0,130},{1,131},{2,132},{3,133},{4,134},{5,135},{6,136},{7,137},{8... | collective-permute-start | bytes 49160 | tf_op jit(solution)/shard_map/ppermute | solution.py:530
  43.5 0.0 collective-permute-done.1.low_ref
  43.5 0.0 collective-permute-done.2.high_ref
  43.5 0.0 copy-done
  43.5 0.8 gather.1
  44.3 0.6 collective-permute-done.6.refs_6_
  44.9 6.0 %collective-permute-done.5.refs_5_ = f32[32,128]{1,0:T(8,128)S(1)} collective-permute-done((f32[32,128]{1,0:T(8,128)S(1)}, f32[32,128]{1,0:T(8,128)S(1)}, u32[]{:S(2)}, u32[]{:S(2)}) %collective-permute-start.5) | collective-permute-done | bytes 16416 | tf_op jit(solution)/shard_map/ppermute | solution.py:530
  51.0 0.0 collective-permute-done.4.refs_4_
  51.0 3.9 %turn.1 = (f32[512,128]{1,0:T(8,128)}, f32[6,32,256]{2,1,0:T(8,128)S(1)}) custom-call(s32[2]{0:T(128)S(1)} %pad_add_fusion.info_ref.refs_0_, f32[64]{0:T(128)S(1)} %bitcast.21, f32[128,256]{1,0:T(8,128)S(1)} %get-tuple-element.29.refs_2_.coef_ref, f32[2,16,128]{2,1,0:T(8,128)S(1)} %get-tuple-element.30.refs_3_, ...), custom_call_target="tpu_custom_call" | custom-call | tf_op jit(solution)/shard_map/turn/pallas_call | solution.py:340
  54.9 5.1 %all-to-all-start.1 = ((f32[64,8,128]{2,1,0:T(8,128)}), f32[64,8,128]{2,1,0:T(8,128)S(1)}, u32[]{:S(2)}, u32[]{:S(2)}) async-start(f32[64,8,128]{2,1,0:T(8,128)} %bitcast.14), calls=%async_computation.1 | async-start | bytes 524288 | tf_op jit(solution)/shard_map/all_to_all | solution.py:568
  60.0 0.1 pad_maximum_fusion.mixrow_ref
  60.1 9.1 %bulk.1 = (f32[2048,128]{1,0:T(8,128)}, f32[2,3,16,128]{3,2,1,0:T(8,128)S(1)}) custom-call(f32[1,128]{1,0:T(1,128)S(1)} %pad_maximum_fusion.mixrow_ref, f32[64]{0:T(128)S(1)} %bitcast.22, f32[16,128,128]{2,1,0:T(8,128)S(1)} %get-tuple-element.24.cells_ref, f32[128,256]{1,0:T(8,128)S(1)} %get-tuple-element.29.refs_2_.coef_ref, ...), custom_call_target="tpu_custom_call" | custom-call | flops 40000000 | bytes 40000000 | tf_op jit(solution)/shard_map/bulk/pallas_call | solution.py:482
  69.2 3.6 %all-to-all-done.1 = f32[64,8,128]{2,1,0:T(8,128)S(1)} async-done(((f32[64,8,128]{2,1,0:T(8,128)}), f32[64,8,128]{2,1,0:T(8,128)S(1)}, u32[]{:S(2)}, u32[]{:S(2)}) %all-to-all-start.1) | async-done | bytes 262176 | tf_op jit(solution)/shard_map/all_to_all | solution.py:568
  72.8 0.2 densify.3
  73.0 0.8 collective-permute-start.7
  73.9 3.1 %collective-permute-done.7 = f32[64,128]{1,0:T(8,128)S(1)} collective-permute-done((f32[64,128]{1,0:T(8,128)S(1)}, f32[64,128]{1,0:T(8,128)S(1)}, u32[]{:S(2)}, u32[]{:S(2)}) %collective-permute-start.7) | collective-permute-done | bytes 32800 | tf_op jit(solution)/shard_map/ppermute | solution.py:530
  77.0 1.4 %collective-permute-start.8 = (f32[64,128]{1,0:T(8,128)S(1)}, f32[64,128]{1,0:T(8,128)S(1)}, u32[]{:S(2)}, u32[]{:S(2)}) collective-permute-start(f32[64,128]{1,0:T(8,128)S(1)} %add.7), channel_id=1, source_target_pairs={{0,128},{1,129},{2,130},{3,131},{4,132},{5,133},{6,134},{7,135},{8... | collective-permute-start | bytes 98312 | tf_op jit(solution)/shard_map/ppermute | solution.py:530
  78.4 1.5 %collective-permute-start.10 = (f32[32,128]{1,0:T(8,128)S(1)}, f32[32,128]{1,0:T(8,128)S(1)}, u32[]{:S(2)}, u32[]{:S(2)}) collective-permute-start(f32[32,128]{1,0:T(8,128)S(1)} %get-tuple-element.41), channel_id=1, source_target_pairs={{0,254},{1,255},{2,128},{3,129},{4,130},{5,131},{6,132},{7,133},{8... | collective-permute-start | bytes 49160 | tf_op jit(solution)/shard_map/ppermute | solution.py:530
  79.9 1.7 %collective-permute-start.9 = (f32[32,128]{1,0:T(8,128)S(1)}, f32[32,128]{1,0:T(8,128)S(1)}, u32[]{:S(2)}, u32[]{:S(2)}) collective-permute-start(f32[32,128]{1,0:T(8,128)S(1)} %get-tuple-element.42), channel_id=1, source_target_pairs={{0,130},{1,131},{2,132},{3,133},{4,134},{5,135},{6,136},{7,137},{8... | collective-permute-start | bytes 49160 | tf_op jit(solution)/shard_map/ppermute | solution.py:530
  81.6 1.5 %collective-permute-done.10.high = f32[32,128]{1,0:T(8,128)S(1)} collective-permute-done((f32[32,128]{1,0:T(8,128)S(1)}, f32[32,128]{1,0:T(8,128)S(1)}, u32[]{:S(2)}, u32[]{:S(2)}) %collective-permute-start.10) | collective-permute-done | bytes 16416 | tf_op jit(solution)/shard_map/ppermute | solution.py:530
  83.1 5.7 %collective-permute-done.9.low = f32[32,128]{1,0:T(8,128)S(1)} collective-permute-done((f32[32,128]{1,0:T(8,128)S(1)}, f32[32,128]{1,0:T(8,128)S(1)}, u32[]{:S(2)}, u32[]{:S(2)}) %collective-permute-start.9) | collective-permute-done | bytes 16416 | tf_op jit(solution)/shard_map/ppermute | solution.py:530
  88.8 0.0 collective-permute-done.8.own
  88.8 1.4 %final.1 = f32[2,64,16,128]{3,2,1,0:T(8,128)} custom-call(s32[2]{0:T(128)S(1)} %pad_add_fusion.info_ref.refs_0_, f32[64]{0:T(128)S(1)} %bitcast.23, f32[128,256]{1,0:T(8,128)S(1)} %get-tuple-element.29.refs_2_.coef_ref, f32[64,128]{1,0:T(8,128)S(1)} %collective-permute-done.8.own, ...), custom_call_target="tpu_custom_call", output_to_operand_aliasing={{}: (7, {})} | custom-call | tf_op jit(solution)/shard_map/final/pallas_call | solution.py:506
  (4 shorter events, 0.0 us)
Async XLA Ops:
  2.3 6.7 %collective-permute-start = (f32[384,128]{1,0:T(8,128)S(1)}, f32[384,128]{1,0:T(8,128)S(1)}, u32[]{:S(2)}, u32[]{:S(2)}) collective-permute-start(f32[384,128]{1,0:T(8,128)S(1)} %get-tuple-element.25), channel_id=1, source_target_pairs={{0,1},{1,0},{2,3},{3,2},{4,5},{5,4},{6,7},{7,6},{8,9},{9,8},{10,11... | collective-permute-start | bytes 589832 | tf_op jit(solution)/shard_map/ppermute | solution.py:530
  3.2 40.3 %copy-start = (f32[1,64]{1,0:T(1,128)S(1)}, f32[1,64]{1,0:T(1,128)}, u32[]{:S(2)}) copy-start(f32[1,64]{1,0:T(1,128)} %param.12) | copy-start | bytes 772
  9.0 25.6 %all-to-all-start = ((f32[576,1,128]{2,1,0:T(1,128)}), f32[576,1,128]{2,1,0:T(1,128)S(1)}, u32[]{:S(2)}, u32[]{:S(2)}) async-start(f32[576,1,128]{2,1,0:T(1,128)} %contrib.1), calls=%async_computation | async-start | bytes 589824 | tf_op jit(solution)/shard_map/all_to_all | solution.py:556
  22.0 21.5 %collective-permute-start.1 = (f32[1032,128]{1,0:T(8,128)}, f32[1032,128]{1,0:T(8,128)S(1)}, u32[]{:S(2)}, u32[]{:S(2)}) collective-permute-start(f32[1032,128]{1,0:T(8,128)} %get-tuple-element.27), channel_id=1, source_target_pairs={{0,126},{1,127},{2,0},{3,1},{4,2},{5,3},{6,4},{7,5},{8,6},{9,7},{1... | collective-permute-start | bytes 1585160 | tf_op jit(solution)/shard_map/ppermute | solution.py:530
  27.0 16.5 %collective-permute-start.2 = (f32[1032,128]{1,0:T(8,128)S(1)}, f32[1032,128]{1,0:T(8,128)S(1)}, u32[]{:S(2)}, u32[]{:S(2)}) collective-permute-start(f32[1032,128]{1,0:T(8,128)S(1)} %get-tuple-element.28), channel_id=1, source_target_pairs={{0,2},{1,3},{2,4},{3,5},{4,6},{5,7},{6,8},{7,9},{8,10},{9,11},{10,... | collective-permute-start | bytes 1585160 | tf_op jit(solution)/shard_map/ppermute | solution.py:530
  34.9 3.9 %collective-permute-start.3 = (f32[64,128]{1,0:T(8,128)S(1)}, f32[64,128]{1,0:T(8,128)S(1)}, u32[]{:S(2)}, u32[]{:S(2)}) collective-permute-start(f32[64,128]{1,0:T(8,128)S(1)} %get-tuple-element.32), channel_id=1, source_target_pairs={{0,1},{1,0},{2,3},{3,2},{4,5},{5,4},{6,7},{7,6},{8,9},{9,8},{10,11... | collective-permute-start | bytes 98312 | tf_op jit(solution)/shard_map/ppermute | solution.py:530
  38.8 12.1 %collective-permute-start.4 = (f32[64,128]{1,0:T(8,128)S(1)}, f32[64,128]{1,0:T(8,128)S(1)}, u32[]{:S(2)}, u32[]{:S(2)}) collective-permute-start(f32[64,128]{1,0:T(8,128)S(1)} %add.6), channel_id=1, source_target_pairs={{0,128},{1,129},{2,130},{3,131},{4,132},{5,133},{6,134},{7,135},{8... | collective-permute-start | bytes 98312 | tf_op jit(solution)/shard_map/ppermute | solution.py:530
  40.2 4.7 %collective-permute-start.6 = (f32[32,128]{1,0:T(8,128)S(1)}, f32[32,128]{1,0:T(8,128)S(1)}, u32[]{:S(2)}, u32[]{:S(2)}) collective-permute-start(f32[32,128]{1,0:T(8,128)S(1)} %get-tuple-element.43), channel_id=1, source_target_pairs={{0,254},{1,255},{2,128},{3,129},{4,130},{5,131},{6,132},{7,133},{8... | collective-permute-start | bytes 49160 | tf_op jit(solution)/shard_map/ppermute | solution.py:530
  42.1 8.9 %collective-permute-start.5 = (f32[32,128]{1,0:T(8,128)S(1)}, f32[32,128]{1,0:T(8,128)S(1)}, u32[]{:S(2)}, u32[]{:S(2)}) collective-permute-start(f32[32,128]{1,0:T(8,128)S(1)} %get-tuple-element.44), channel_id=1, source_target_pairs={{0,130},{1,131},{2,132},{3,133},{4,134},{5,135},{6,136},{7,137},{8... | collective-permute-start | bytes 49160 | tf_op jit(solution)/shard_map/ppermute | solution.py:530
  54.9 17.9 %all-to-all-start.1 = ((f32[64,8,128]{2,1,0:T(8,128)}), f32[64,8,128]{2,1,0:T(8,128)S(1)}, u32[]{:S(2)}, u32[]{:S(2)}) async-start(f32[64,8,128]{2,1,0:T(8,128)} %bitcast.14), calls=%async_computation.1 | async-start | bytes 524288 | tf_op jit(solution)/shard_map/all_to_all | solution.py:568
  73.0 3.9 %collective-permute-start.7 = (f32[64,128]{1,0:T(8,128)S(1)}, f32[64,128]{1,0:T(8,128)S(1)}, u32[]{:S(2)}, u32[]{:S(2)}) collective-permute-start(f32[64,128]{1,0:T(8,128)S(1)} %densify.3), channel_id=1, source_target_pairs={{0,1},{1,0},{2,3},{3,2},{4,5},{5,4},{6,7},{7,6},{8,9},{9,8},{10,11... | collective-permute-start | bytes 98312 | tf_op jit(solution)/shard_map/ppermute | solution.py:530
  77.0 11.8 %collective-permute-start.8 = (f32[64,128]{1,0:T(8,128)S(1)}, f32[64,128]{1,0:T(8,128)S(1)}, u32[]{:S(2)}, u32[]{:S(2)}) collective-permute-start(f32[64,128]{1,0:T(8,128)S(1)} %add.7), channel_id=1, source_target_pairs={{0,128},{1,129},{2,130},{3,131},{4,132},{5,133},{6,134},{7,135},{8... | collective-permute-start | bytes 98312 | tf_op jit(solution)/shard_map/ppermute | solution.py:530
  78.4 4.7 %collective-permute-start.10 = (f32[32,128]{1,0:T(8,128)S(1)}, f32[32,128]{1,0:T(8,128)S(1)}, u32[]{:S(2)}, u32[]{:S(2)}) collective-permute-start(f32[32,128]{1,0:T(8,128)S(1)} %get-tuple-element.41), channel_id=1, source_target_pairs={{0,254},{1,255},{2,128},{3,129},{4,130},{5,131},{6,132},{7,133},{8... | collective-permute-start | bytes 49160 | tf_op jit(solution)/shard_map/ppermute | solution.py:530
  79.9 8.9 %collective-permute-start.9 = (f32[32,128]{1,0:T(8,128)S(1)}, f32[32,128]{1,0:T(8,128)S(1)}, u32[]{:S(2)}, u32[]{:S(2)}) collective-permute-start(f32[32,128]{1,0:T(8,128)S(1)} %get-tuple-element.42), channel_id=1, source_target_pairs={{0,130},{1,131},{2,132},{3,133},{4,134},{5,135},{6,136},{7,137},{8... | collective-permute-start | bytes 49160 | tf_op jit(solution)/shard_map/ppermute | solution.py:530
